TPU v7x, 128 devices: a whole 4x4x4 slice. The times are simulated.
128 devices in a mesh: mode: 8 (over z, core), rad: 16 (over x, y).
Axes of the slice: x: 4, y: 4, z: 4, core: 2. Of those that a mesh axis runs over, the one named last changes fastest.
Arguments:
- field_coef: float32 [32, 2048, 384], P('mode', 'rad'), may hold values from -6 to 6
- prior_forcing: float32 [32, 2048, 384], P('mode', 'rad'), may hold values from -4 to 4
- base_flow: float32 [384, 1024], P('rad'), may hold values from 0.2 to 2
- keep_modes: int32 [32], P('mode'), may hold values from 256 to 341, as said below
- owner_band: int32 [262144, 1], P(('mode', 'rad')), may hold values from 0 to 15; in each aligned block of 2048 rows (0 to 2047, 2048 to 4095, ...) at most 256 rows name the same one
- cell_index: int32 [262144], P(('mode', 'rad')), may hold values from 0 to 3071
- axial_pos: float32 [262144], P(('mode', 'rad')), may hold values from 0 to 40
- particle_vel: float32 [262144], P(('mode', 'rad')), may hold values from -6 to 6
- response_rate: float32 [262144], P(('mode', 'rad')), may hold values from 0.5 to 4
- particle_mass: float32 [262144], P(('mode', 'rad')), may hold values from 0.5 to 5
Outputs:
- field_next: float32 [32, 2048, 384], P('mode', 'rad')
- forcing: float32 [32, 2048, 384], P('mode', 'rad')
Inputs may be any that keep to these rules, and one draw needn't show every extreme that they name: Each axial mode k keeps azimuthal wavenumbers up to keep_modes[k]; the largest and the smallest allowed values both occur. `owner_band`: in the rows of one device no band is named by more than 256 particles, a bound that some block reaches. A particle's cell lies at radial offset cell_index // 128 in its owner band and angular offset cell_index % 128 in the angle block of its device's mode index.
All inputs are finite; a program needn't handle non-finite values.
Results may differ from a plain program's by a relative error of at most 0.0003.
Values sent between devices are 32-bit elements; how exact they have to be, the bound alone decides.
A program may use at most 64 MiB of HBM per device.

v0:
```python
import math

import jax
import jax.numpy as jnp
import ml_dtypes
import numpy as np
from jax import lax
from jax.experimental import pallas as pl
from jax.experimental.pallas import tpu as pltpu
from jax.sharding import PartitionSpec as P

time_step = 0.5
viscosity = 0.0004
alpha_rk = 1.0 / 15.0
beta_rk = 1.0 / 15.0
gamma_rk = 5.0 / 12.0
zeta_rk = -17.0 / 60.0

RADII = 384
AZIM = 1024
HALF = 512
KZ = 32
P_DEV = 2048
BAND = 24
ARC = 128
CAP = 256
MODES = 8
RADS = 16
KL = 4
ROWS = BAND * KL
F32 = jnp.float32
BF16 = jnp.bfloat16
MESH = pl.DeviceIdType.MESH
implicit = beta_rk * time_step * viscosity
VMEM = pltpu.VMEM


def fourier_half():
    i = np.arange(AZIM)
    m = np.where(i <= HALF, i, i - HALF)
    t = np.arange(HALF)
    angle = 2.0 * math.pi * ((t[None, :] * m[:, None]) % AZIM) / AZIM
    scale = np.where((m == 0) | (i == HALF), math.sqrt(1.0 / AZIM), math.sqrt(2.0 / AZIM))
    table = (np.where((i > HALF)[:, None], np.sin(angle), np.cos(angle)) * scale[:, None]).astype(
        np.float32
    )
    high = table.astype(ml_dtypes.bfloat16)
    low = (table - high.astype(np.float32)).astype(ml_dtypes.bfloat16)
    return high, low


def split(x):
    high = x.astype(BF16)
    return high, (x - high.astype(F32)).astype(BF16)


def mm(a, b):
    return lax.dot_general(a, b, (((1,), (0,)), ((), ())), preferred_element_type=F32)


def mm_nt(a, b):
    return lax.dot_general(a, b, (((1,), (1,)), ((), ())), preferred_element_type=F32)


def iota(shape, dim):
    return lax.broadcasted_iota(jnp.int32, shape, dim)


def greet(mode_peers, rad_peers):
    barrier = pltpu.get_barrier_semaphore()
    mode, rad = lax.axis_index("mode"), lax.axis_index("rad")
    if rad_peers:
        for d in range(1, RADS):
            pl.semaphore_signal(
                barrier, inc=1, device_id=(mode, lax.rem(rad + d, RADS)), device_id_type=MESH
            )
    if mode_peers:
        for d in range(1, MODES):
            pl.semaphore_signal(
                barrier, inc=1, device_id=(lax.rem(mode + d, MODES), rad), device_id_type=MESH
            )
    return barrier, (RADS - 1) * rad_peers + (MODES - 1) * mode_peers


def push_copy(src, dst, send, recv, mode, rad):
    return pltpu.make_async_remote_copy(
        src_ref=src,
        dst_ref=dst,
        send_sem=send,
        recv_sem=recv,
        device_id=(mode, rad),
        device_id_type=MESH,
    )


def radial_tiles(shape, dims):
    j = iota(shape, dims[0])
    sub = iota(shape, dims[1])
    return jnp.where(sub < 4, j, RADII - 1 - j), sub


def factor(mode, rad, diag_ref, edge_ref, g_ref):
    shape = (RADII // 2, 8, 128)
    r, sub = radial_tiles(shape, (0, 1))
    off = r.astype(F32)
    inverse = (RADII * RADII) / (off + 0.5)
    last = r == RADII - 1
    lower = off * inverse
    upper = jnp.where(last, 0.0, (off + 1.0) * inverse)
    centre = -(off + (off + 1.0) * jnp.where(last, 2.0, 1.0)) * inverse
    k = mode * KL + sub % KL
    kappa = 0.5 + 1.5 * k.astype(F32) / KZ
    coef = lax.rem(rad, 8) * 128 + iota(shape, 2)
    m = jnp.where(coef <= HALF, coef, coef - HALF).astype(F32)
    unit = (off + 0.5) / RADII
    diagonal = centre - m * m / (unit * unit) - kappa * kappa
    diag_ref[...] = 1.0 - implicit * diagonal
    top = sub < 4
    before = jnp.where(top, off - 1.0, off + 1.0)
    before_inverse = (RADII * RADII) / (before + 0.5)
    inward = jnp.where(top, (before + 1.0) * before_inverse, before * before_inverse)
    outward = jnp.where(top, lower, upper)
    edge_ref[...] = jnp.where(
        (r == 0) | last, 0.0, (implicit * implicit) * inward * outward
    )

    def step(j, g):
        g = 1.0 / (diag_ref[j] - edge_ref[j] * g)
        g_ref[j] = g
        return g

    lax.fori_loop(0, RADII // 2, step, jnp.zeros((8, 128), F32))


def dispatch(own, cell, pos, vel, rate, mass, fields_ref):
    owner = own[...]
    bands = iota((RADS, P_DEV), 0)
    match = (bands == owner).astype(F32)
    match_bf = match.astype(BF16)
    chunk = 256
    tri = (iota((chunk, chunk), 0) < iota((chunk, chunk), 1)).astype(F32).astype(BF16)
    running = jnp.zeros((RADS, 1), F32)
    places = []
    for n in range(P_DEV // chunk):
        part = match[:, n * chunk : (n + 1) * chunk]
        ahead = mm(match_bf[:, n * chunk : (n + 1) * chunk], tri) + running
        places.append(jnp.sum(ahead * part, axis=0, keepdims=True))
        running = running + jnp.sum(part, axis=1, keepdims=True)
    place = jnp.concatenate(places, axis=1).astype(jnp.int32)
    slots = (iota((CAP, P_DEV), 0) == place).astype(F32).astype(BF16)
    cells = cell[...]
    pieces = [(cells // ARC).astype(F32), (cells % ARC).astype(F32)]
    for ref in (pos, vel, rate, mass):
        left = ref[...]
        for _ in range(3):
            piece = left.astype(BF16).astype(F32)
            pieces.append(piece)
            left = left - piece
    rows = jnp.concatenate([jnp.where(match > 0.5, p, 0.0) for p in pieces], axis=0).astype(BF16)
    sorted_rows = mm_nt(rows, slots)

    def take(n):
        return sorted_rows[n * RADS : (n + 1) * RADS]

    fields_ref[:, 0, :] = take(0) * ARC + take(1)
    for f in range(4):
        fields_ref[:, 1 + f, :] = take(2 + 3 * f) + take(3 + 3 * f) + take(4 + 3 * f)
    for f in range(5, 8):
        fields_ref[:, f, :] = jnp.zeros((RADS, CAP), F32)


def k1_body(
    field, own, cell, pos, vel, rate, mass,
    pieces, gathered, arrived, g_ref,
    outgoing, fields, diag, edge,
    fsend, frecv, psend, precv, gsend, grecv,
):
    mode, rad = lax.axis_index("mode"), lax.axis_index("rad")
    barrier, count = greet(True, True)
    dispatch(own, cell, pos, vel, rate, mass, fields)
    pl.semaphore_wait(barrier, count)

    def peer(d):
        return lax.rem(rad + d, RADS)

    def particle_copy(d):
        return push_copy(
            fields.at[peer(d)], arrived.at[rad], psend.at[d], precv.at[d], mode, peer(d)
        )

    def field_copy(d):
        return push_copy(
            outgoing.at[pl.ds(pl.multiple_of(peer(d) * ROWS, 8), ROWS)],
            pieces.at[pl.ds(pl.multiple_of(rad * ROWS, 8), ROWS)],
            fsend.at[d], frecv.at[d], mode, peer(d),
        )

    def gather_copy(d):
        other = lax.rem(mode + d, MODES)
        return push_copy(
            gathered.at[mode], gathered.at[mode], gsend.at[d], grecv.at[d], other, rad
        )

    for d in range(1, RADS):
        particle_copy(d).start()
    for k in range(KL):
        outgoing[pl.ds(k, RADII, stride=KL), :] = jnp.transpose(field[k])
    for d in range(1, RADS):
        field_copy(d).start()
    arrived[rad] = fields[rad]
    own_rows = pl.ds(pl.multiple_of(rad * ROWS, 8), ROWS)
    pieces[own_rows, :] = outgoing[own_rows, :]
    for d in range(1, RADS):
        particle_copy(d).wait_recv()
    gathered[mode, 0:RADS, :] = arrived[:, 0, :]
    gathered[mode, RADS : 2 * RADS, :] = arrived[:, 1, :]
    for d in range(1, MODES):
        gather_copy(d).start()
    factor(mode, rad, diag, edge, g_ref)
    for d in range(1, RADS):
        particle_copy(d).wait_send()
        field_copy(d).wait()
    for d in range(1, MODES):
        gather_copy(d).wait()


def cell_parts(cells):
    r = jnp.floor(cells * (1.0 / ARC))
    half = jnp.where(r >= BAND // 2, 1.0, 0.0)
    rh = r - half * (BAND // 2)
    pair = jnp.floor(rh * 0.5)
    column = cells + (half - r) * ARC
    return column.astype(jnp.int32), pair.astype(jnp.int32), (rh - 2.0 * pair).astype(jnp.int32)


def axial_rows(mode, positions, parity):
    sub = iota((8, 1), 0)
    k = mode * KL + sub % KL
    kappa = 0.5 + 1.5 * k.astype(F32) / KZ
    phases = kappa * positions
    chosen = (sub // KL) == parity
    scaling = 1.0 / math.sqrt(KZ)
    return (
        jnp.where(chosen, jnp.cos(phases) * scaling, 0.0),
        jnp.where(chosen, -jnp.sin(phases) * scaling, 0.0),
    )


PAIRS = BAND // 4


def k2_body(pieces, gathered, table_hi, table_lo, grid, partial):
    mode = lax.axis_index("mode")
    sign = jnp.where(iota((1, AZIM), 1) % 2 == 0, 1.0, -1.0)
    for c in range(2):
        x = jnp.concatenate(
            [pieces[(c * 8 + ib) * ROWS : (c * 8 + ib + 1) * ROWS, :] for ib in range(8)], axis=1
        )
        hi, lo = split(jnp.concatenate([x, x * sign], axis=0))
        for n in range(2):
            cols = slice(n * 256, (n + 1) * 256)
            th, tl = table_hi[:, cols], table_lo[:, cols]
            out = mm(hi, th) + mm(lo, th) + mm(hi, tl)
            for half in range(2):
                for a in range(2):
                    grid[half * 4 + n * 2 + a, c * ROWS : (c + 1) * ROWS, :] = out[
                        half * ROWS : (half + 1) * ROWS, a * 128 : (a + 1) * 128
                    ]

    def arc(m, carry):
        stack = []
        for c in range(2):
            lower = grid[m, c * ROWS : c * ROWS + 48, :]
            upper = grid[m, c * ROWS + 48 : (c + 1) * ROWS, :]
            stack.append(jnp.concatenate([lower, upper], axis=1))
        hi, lo = split(jnp.concatenate(stack, axis=0))
        lhs = jnp.concatenate([hi, lo], axis=0)
        for s in range(RADS):
            column, pair, parity = cell_parts(gathered[m, s : s + 1, :])
            onehot = (iota((256, CAP), 0) == column).astype(F32).astype(BF16)
            both = mm(lhs, onehot)
            values = both[:96] + both[96:]
            weights = axial_rows(mode, gathered[m, RADS + s : RADS + s + 1, :], parity)
            total = jnp.zeros((8, CAP), F32)
            for c in range(2):
                taken = jnp.zeros((8, CAP), F32)
                for q in range(PAIRS):
                    row = c * 48 + q * 8
                    taken = jnp.where(pair == q, values[row : row + 8], taken)
                total = total + taken * weights[c]
            partial[m, s : s + 1, :] = jnp.sum(total, axis=0, keepdims=True)
        return carry

    lax.fori_loop(0, MODES, arc, 0)


def k3_body(partial, arrived, pushes, parts, rsend, rrecv, gsend, grecv):
    mode, rad = lax.axis_index("mode"), lax.axis_index("rad")
    barrier, count = greet(True, False)
    pl.semaphore_wait(barrier, count)

    def reduce_copy(d):
        other = lax.rem(mode + d, MODES)
        return push_copy(
            partial.at[other], parts.at[mode], rsend.at[d], rrecv.at[d], other, rad
        )

    def gather_copy(d):
        other = lax.rem(mode + d, MODES)
        return push_copy(
            pushes.at[mode], pushes.at[mode], gsend.at[d], grecv.at[d], other, rad
        )

    for d in range(1, MODES):
        reduce_copy(d).start()
    parts[mode] = partial[mode]
    for d in range(1, MODES):
        reduce_copy(d).wait_recv()
    fluid = parts[0]
    for n in range(1, MODES):
        fluid = fluid + parts[n]
    relative = (fluid - arrived[:, 2, :]) * arrived[:, 3, :]
    pushes[mode] = -arrived[:, 4, :] * relative
    for d in range(1, MODES):
        gather_copy(d).start()
    for d in range(1, MODES):
        reduce_copy(d).wait_send()
        gather_copy(d).wait()


def k4_body(grid, gathered, pushes, base, table_hi, table_lo, spectral, terms, onehots, masses):
    mode = lax.axis_index("mode")

    def arc(m, carry):
        for s in range(RADS):
            lanes = slice(s * CAP, (s + 1) * CAP)
            column, pair, parity = cell_parts(gathered[m, s : s + 1, :])
            onehots[:, lanes] = (iota((256, CAP), 0) == column).astype(F32).astype(BF16)
            weights = axial_rows(mode, gathered[m, RADS + s : RADS + s + 1, :], parity)
            push = pushes[m, s : s + 1, :]
            rows = []
            lows = []
            for c in range(2):
                value = push * weights[c]
                high = value.astype(BF16).astype(F32)
                low = value - high
                for q in range(PAIRS):
                    rows.append(jnp.where(pair == q, high, 0.0))
                    lows.append(jnp.where(pair == q, low, 0.0))
            masses[:, lanes] = jnp.concatenate(rows + lows, axis=0).astype(BF16)
        both = mm_nt(masses[...], onehots[...])
        deposit = both[:96] + both[96:]
        for h in range(2):
            speed = base[m, h * 48 : (h + 1) * 48, :]
            cols = slice(h * 128, (h + 1) * 128)
            real = grid[m, h * 48 : (h + 1) * 48, :]
            imag = grid[m, ROWS + h * 48 : ROWS + (h + 1) * 48, :]
            terms[m, h * 48 : (h + 1) * 48, :] = speed * imag + deposit[:48, cols]
            terms[m, ROWS + h * 48 : ROWS + (h + 1) * 48, :] = deposit[48:, cols] - speed * real
        return carry

    lax.fori_loop(0, MODES, arc, 0)
    first = jnp.concatenate([terms[a] for a in range(4)], axis=1)
    second = jnp.concatenate([terms[a + 4] for a in range(4)], axis=1)
    hi, lo = split(jnp.concatenate([first + second, first - second], axis=0))
    even = iota((1, 128), 1) % 2 == 0
    for ib in (0, 1, 2, 4, 5, 6):
        th, tl = table_hi[ib * 128 : (ib + 1) * 128, :], table_lo[ib * 128 : (ib + 1) * 128, :]
        out = mm_nt(hi, th) + mm_nt(lo, th) + mm_nt(hi, tl)
        chosen = jnp.where(even, out[: 2 * ROWS], out[2 * ROWS :])
        spectral[ib * ROWS : (ib + 1) * ROWS, :] = chosen[:ROWS]
        spectral[(8 + ib) * ROWS : (9 + ib) * ROWS, :] = chosen[ROWS:]
    for ib in (3, 7, 11, 15):
        spectral[ib * ROWS : (ib + 1) * ROWS, :] = jnp.zeros((ROWS, 128), F32)


def k5_body(spectral, returned, send, recv):
    mode, rad = lax.axis_index("mode"), lax.axis_index("rad")
    barrier, count = greet(False, True)
    pl.semaphore_wait(barrier, count)
    takes = lax.rem(rad, 4) != 3

    def rows(n):
        return pl.ds(pl.multiple_of(n * ROWS, 8), ROWS)

    def copy(d):
        other = lax.rem(rad + d, RADS)
        return push_copy(
            spectral.at[rows(other)], returned.at[rows(rad)], send.at[d], recv.at[d], mode, other
        )

    for d in range(1, RADS):
        @pl.when(lax.rem(lax.rem(rad + d, RADS), 4) != 3)
        def _():
            copy(d).start()

    @pl.when(takes)
    def _():
        returned[rows(rad), :] = spectral[rows(rad), :]

    @pl.when(jnp.logical_not(takes))
    def _():
        returned[...] = jnp.zeros_like(returned)

    for d in range(1, RADS):
        @pl.when(lax.rem(lax.rem(rad + d, RADS), 4) != 3)
        def _():
            copy(d).wait_send()

        @pl.when(takes)
        def _():
            copy(d).wait_recv()


def band_rows(n):
    off = iota((1, RADII), 1).astype(F32)
    inverse = (RADII * RADII) / (off + 0.5)
    last = off == RADII - 1
    lower = off * inverse
    upper = jnp.where(last, 0.0, (off + 1.0) * inverse)
    centre = -(off + (off + 1.0) * jnp.where(last, 2.0, 1.0)) * inverse
    radius = (off + 0.5) / RADII
    return lower, upper, centre, radius * radius


def k6_body(returned, field, prior, keep, g_ref, nxt, forcing, rhs, work, coupling):
    mode, rad = lax.axis_index("mode"), lax.axis_index("rad")
    lower, upper, centre, radius_sq = band_rows(RADII)
    coef = lax.rem(rad, 8) * 128 + iota((128, 1), 0)
    m_col = jnp.where(coef <= HALF, coef, coef - HALF)
    wave_sq = m_col.astype(F32) * m_col.astype(F32)
    lane = lax.rem(rad, 8) * 128 + iota((1, 128), 1)
    m_row = jnp.where(lane <= HALF, lane, lane - HALF)
    for k in range(KL):
        kappa = 0.5 + 1.5 * (mode * KL + k).astype(F32) / KZ
        f = field[k]
        diagonal = centre - wave_sq / radius_sq - kappa * kappa
        laplace = lower * pltpu.roll(f, 1, 1) + diagonal * f + upper * pltpu.roll(f, RADII - 1, 1)
        known = f + time_step * (alpha_rk * viscosity * laplace + zeta_rk * prior[k])
        raw = returned[pl.ds(k, RADII, stride=KL), :]
        kept = jnp.where(m_row <= keep[k], raw, 0.0)
        forcing[k] = jnp.transpose(kept)
        rhs[pl.ds(k, RADII, stride=KL), :] = jnp.transpose(known) + (time_step * gamma_rk) * kept
    half = RADII // 2
    shape = (half, 8, 128)
    r, sub = radial_tiles(shape, (0, 1))
    off = r.astype(F32)
    scaled = implicit * (RADII * RADII) / (off + 0.5)
    inner = -scaled * jnp.where(sub < 4, off + 1.0, off)
    outer = -scaled * jnp.where(sub < 4, off, jnp.where(r == RADII - 1, 0.0, off + 1.0))
    g = g_ref[...]
    top_tile = iota((8, 128), 0) < 4

    def fold(q, carry):
        upper_rows = rhs[pl.ds(pl.multiple_of(q * 8, 8), 8), :]
        lower_rows = rhs[pl.ds(pl.multiple_of((half - 1 - q) * 8, 8), 8), :]
        work[2 * q] = jnp.where(top_tile, upper_rows, lower_rows)
        work[2 * q + 1] = pltpu.roll(jnp.where(top_tile, lower_rows, upper_rows), 4, 0)
        return carry

    lax.fori_loop(0, half // 2, fold, 0, unroll=4)
    work[...] = work[...] * g
    coupling[...] = outer * g

    def down(j, d):
        d = work[j] - coupling[j] * d
        work[j] = d
        return d

    d = lax.fori_loop(0, half, down, jnp.zeros((8, 128), F32), unroll=8)
    coupling[...] = inner * g
    v = coupling[half - 1]
    x = (d - v * pltpu.roll(d, 4, 0)) / (1.0 - v * pltpu.roll(v, 4, 0))
    work[half - 1] = x

    def back(n, x):
        j = half - 2 - n
        x = work[j] - coupling[j] * x
        work[j] = x
        return x

    lax.fori_loop(0, half - 1, back, x, unroll=8)

    def unfold(q, carry):
        even = work[2 * q]
        odd = pltpu.roll(work[2 * q + 1], 4, 0)
        rhs[pl.ds(pl.multiple_of(q * 8, 8), 8), :] = jnp.where(top_tile, even, odd)
        rhs[pl.ds(pl.multiple_of((half - 1 - q) * 8, 8), 8), :] = jnp.where(top_tile, odd, even)
        return carry

    lax.fori_loop(0, half // 2, unfold, 0, unroll=4)
    for k in range(KL):
        nxt[k] = jnp.transpose(rhs[pl.ds(k, RADII, stride=KL), :])


def vmem_call(body, outs, n_in, scratch, collective=None, smem=(), name=None):
    spec = [
        pl.BlockSpec(memory_space=pltpu.SMEM if n in smem else VMEM) for n in range(n_in)
    ]
    params = dict(vmem_limit_bytes=56 * 1024 * 1024)
    if collective is not None:
        params.update(collective_id=collective, has_side_effects=True)
    return pl.pallas_call(
        body,
        out_shape=[jax.ShapeDtypeStruct(s, F32) for s in outs],
        in_specs=spec,
        out_specs=[pl.BlockSpec(memory_space=VMEM)] * len(outs),
        scratch_shapes=scratch,
        compiler_params=pltpu.CompilerParams(**params),
        name=name,
    )


DMA = pltpu.SemaphoreType.DMA


def per_device(
    field_coef,
    prior_forcing,
    base_flow,
    keep_modes,
    owner_band,
    cell_index,
    axial_pos,
    particle_vel,
    response_rate,
    particle_mass,
):
    mode = lax.axis_index("mode")
    high, low = fourier_half()
    table_hi, table_lo = jnp.asarray(high), jnp.asarray(low)
    kappa = 0.5 + 1.5 * (mode * KL + jnp.arange(KL)).astype(F32) / KZ
    speed = base_flow[:, None, :] * kappa[None, :, None]
    speed = speed.reshape(ROWS, MODES, ARC).transpose(1, 0, 2)

    def row(x):
        return x.reshape(1, P_DEV)

    pieces, gathered, arrived, g = vmem_call(
        k1_body,
        [(RADS * ROWS, 128), (MODES, 2 * RADS, CAP), (RADS, 8, CAP), (RADII // 2, 8, 128)],
        7,
        [
            VMEM((RADS * ROWS, 128), F32),
            VMEM((RADS, 8, CAP), F32),
            VMEM((RADII // 2, 8, 128), F32),
            VMEM((RADII // 2, 8, 128), F32),
            DMA((RADS,)), DMA((RADS,)), DMA((RADS,)), DMA((RADS,)),
            DMA((MODES,)), DMA((MODES,)),
        ],
        collective=0,
        name="exchange",
    )(
        field_coef, row(owner_band), row(cell_index), row(axial_pos), row(particle_vel),
        row(response_rate), row(particle_mass),
    )
    grid, partial = vmem_call(
        k2_body,
        [(MODES, 2 * ROWS, 128), (MODES, RADS, CAP)],
        4,
        [],
        name="sample",
    )(pieces, gathered, table_hi, table_lo)
    (pushes,) = vmem_call(
        k3_body,
        [(MODES, RADS, CAP)],
        2,
        [VMEM((MODES, RADS, CAP), F32), DMA((MODES,)), DMA((MODES,)), DMA((MODES,)), DMA((MODES,))],
        collective=1,
        name="push",
    )(partial, arrived)
    (spectral,) = vmem_call(
        k4_body,
        [(RADS * ROWS, 128)],
        6,
        [
            VMEM((MODES, 2 * ROWS, 128), F32),
            VMEM((256, RADS * CAP), BF16),
            VMEM((192, RADS * CAP), BF16),
        ],
        name="deposit",
    )(grid, gathered, pushes, speed, table_hi, table_lo)
    (returned,) = vmem_call(
        k5_body,
        [(RADS * ROWS, 128)],
        1,
        [DMA((RADS,)), DMA((RADS,))],
        collective=2,
        name="give_back",
    )(spectral)
    field_next, forcing = vmem_call(
        k6_body,
        [(KL, 128, RADII), (KL, 128, RADII)],
        5,
        [
            VMEM((RADS * ROWS, 128), F32),
            VMEM((RADII // 2, 8, 128), F32),
            VMEM((RADII // 2, 8, 128), F32),
        ],
        smem=(3,),
        name="solve",
    )(returned, field_coef, prior_forcing, keep_modes, g)
    return (field_next, forcing)


def solution(mesh):
    in_specs = (
        P("mode", "rad", None),
        P("mode", "rad", None),
        P("rad", None),
        P("mode"),
        P(("mode", "rad"), None),
        P(("mode", "rad")),
        P(("mode", "rad")),
        P(("mode", "rad")),
        P(("mode", "rad")),
        P(("mode", "rad")),
    )
    out_specs = (P("mode", "rad", None), P("mode", "rad", None))
    return jax.shard_map(
        per_device, mesh=mesh, in_specs=in_specs, out_specs=out_specs, check_vma=False
    )
```

profile of v0, /device:TPU:1, one launch (start us, length us, event | category | flops | bytes accessed | tf_op | source)
XLA Modules:
  0.0 93.9 jit_solution(4124296992257325847)
XLA Ops:
  0.6 27.5 %exchange.1 = (f32[1536,128]{1,0:T(8,128)}, f32[8,32,256]{2,1,0:T(8,128)}, f32[16,8,256]{2,1,0:T(8,128)}, f32[192,8,128]{2,1,0:T(8,128)}) custom-call(f32[4,128,384]{2,1,0:T(8,128)} %field.3, s32[1,2048]{1,0:T(1,128)} %bitcast.8, s32[1,2048]{1,0:T(1,128)} %bitcast.9, f32[1,2048]{1,0:T(1,128)} %bitcast.10, f32[1,2048]{1,0:T(1,128)} %bitcast.11, ...), custom_call_target="tpu_custom_call" | custom-call | tf_op jit(solution)/shard_map/exchange/pallas_call | solution.py:539
  28.1 14.7 %sample.1 = (f32[8,192,128]{2,1,0:T(8,128)}, f32[8,16,256]{2,1,0:T(8,128)}) custom-call(f32[1536,128]{1,0:T(8,128)} %get-tuple-element.8.pieces, f32[8,32,256]{2,1,0:T(8,128)} %get-tuple-element.9.gathered, bf16[1024,512]{1,0:T(8,128)(2,1)} %constant.19.clone.table_hi, bf16[1024,512]{1,0:T(8,128)(2,1)} %constant.20.clone.table_lo), custom_call_target="tpu_custom_call" | custom-call | tf_op jit(solution)/shard_map/sample/pallas_call | solution.py:557
  42.8 0.0 copy-start
  42.8 11.3 %push.1.pushes = f32[8,16,256]{2,1,0:T(8,128)} custom-call(f32[8,16,256]{2,1,0:T(8,128)} %get-tuple-element.11.partial, f32[16,8,256]{2,1,0:T(8,128)} %get-tuple-element.12.arrived), custom_call_target="tpu_custom_call" | custom-call | tf_op jit(solution)/shard_map/push/pallas_call | solution.py:564
  54.1 0.0 copy-done
  54.2 0.1 mul.25
  54.3 0.2 mul.26
  54.5 0.1 mul.29
  54.6 0.9 fusion.base
  55.4 15.3 %deposit.1.spectral = f32[1536,128]{1,0:T(8,128)} custom-call(f32[8,192,128]{2,1,0:T(8,128)} %get-tuple-element.10.grid, f32[8,32,256]{2,1,0:T(8,128)} %get-tuple-element.9.gathered, f32[8,16,256]{2,1,0:T(8,128)} %push.1.pushes, f32[8,96,128]{2,1,0:T(8,128)} %fusion.base, bf16[1024,512]{1,0:T(8,128)(2,1)} %constant.19.clone.table_hi, ...), custom_call_target="tpu_custom_call" | custom-call | tf_op jit(solution)/shard_map/deposit/pallas_call | solution.py:572
  70.8 16.8 %give_back.1.returned = f32[1536,128]{1,0:T(8,128)} custom-call(f32[1536,128]{1,0:T(8,128)} %deposit.1.spectral), custom_call_target="tpu_custom_call" | custom-call | tf_op jit(solution)/shard_map/give_back/pallas_call | solution.py:583
  87.6 6.3 %solve.1 = (f32[4,128,384]{2,1,0:T(8,128)}, f32[4,128,384]{2,1,0:T(8,128)}) custom-call(f32[1536,128]{1,0:T(8,128)} %give_back.1.returned, f32[4,128,384]{2,1,0:T(8,128)} %field.3, f32[4,128,384]{2,1,0:T(8,128)} %prior.1, s32[4]{0:T(128)} %keep.1, f32[192,8,128]{2,1,0:T(8,128)} %get-tuple-element.13.g_ref), custom_call_target="tpu_custom_call" | custom-call | tf_op jit(solution)/shard_map/solve/pallas_call | solution.py:591
  (2 shorter events, 0.0 us)
Async XLA Ops:
  42.8 11.4 %copy-start = (f32[24,1024]{1,0:T(8,128)S(1)}, f32[24,1024]{1,0:T(8,128)}, u32[]{:S(2)}) copy-start(f32[24,1024]{1,0:T(8,128)} %param.14) | copy-start | bytes 294916
where the time goes:
time: 94.1 us; the launch traced here: 93.9 us
  Pallas kernels  92 us (98%)
    pallas_call x1, Pallas kernels, per_device(): vmem_call(k1_body, [(RADS * ROWS, 128), (MODES, 2 * RADS, CAP), (RADS, 8,...  27.5 us
    pallas_call x1, Pallas kernels, per_device(): vmem_call(k5_body, [(RADS * ROWS, 128)], 1, [DMA((RADS,)), DMA((RADS,))],...  16.8 us
    pallas_call x1, Pallas kernels, per_device(): vmem_call(k4_body, [(RADS * ROWS, 128)], 6, [VMEM((MODES, 2 * ROWS, 128),...  15.3 us
    pallas_call x1, Pallas kernels, per_device(): vmem_call(k2_body, [(MODES, 2 * ROWS, 128), (MODES, RADS, CAP)], 4, [], n...  14.7 us
    pallas_call x1, Pallas kernels, per_device(): vmem_call(k3_body, [(MODES, RADS, CAP)], 2, [VMEM((MODES, RADS, CAP), F32...  11.3 us
    pallas_call x1, Pallas kernels, per_device(): vmem_call(k6_body, [(KL, 128, RADII), (KL, 128, RADII)], 5, [VMEM((RADS *...  6.3 us

commit v1 on v0

v1 whole, which is shorter than its diff:
```python
import math

import jax
import jax.numpy as jnp
import ml_dtypes
import numpy as np
from jax import lax
from jax.experimental import pallas as pl
from jax.experimental.pallas import tpu as pltpu
from jax.sharding import PartitionSpec as P

time_step = 0.5
viscosity = 0.0004
alpha_rk = 1.0 / 15.0
beta_rk = 1.0 / 15.0
gamma_rk = 5.0 / 12.0
zeta_rk = -17.0 / 60.0

RADII = 384
AZIM = 1024
HALF = 512
KZ = 32
P_DEV = 2048
BAND = 24
ARC = 128
CAP = 256
MODES = 8
RADS = 16
KL = 4
ROWS = BAND * KL
F32 = jnp.float32
BF16 = jnp.bfloat16
MESH = pl.DeviceIdType.MESH
implicit = beta_rk * time_step * viscosity
VMEM = pltpu.VMEM


def fourier_half():
    i = np.arange(AZIM)
    m = np.where(i <= HALF, i, i - HALF)
    t = np.arange(HALF)
    angle = 2.0 * math.pi * ((t[None, :] * m[:, None]) % AZIM) / AZIM
    scale = np.where((m == 0) | (i == HALF), math.sqrt(1.0 / AZIM), math.sqrt(2.0 / AZIM))
    table = (np.where((i > HALF)[:, None], np.sin(angle), np.cos(angle)) * scale[:, None]).astype(
        np.float32
    )
    high = table.astype(ml_dtypes.bfloat16)
    low = (table - high.astype(np.float32)).astype(ml_dtypes.bfloat16)
    return high, low


def split(x):
    high = x.astype(BF16)
    return high, (x - high.astype(F32)).astype(BF16)


def mm(a, b):
    return lax.dot_general(a, b, (((1,), (0,)), ((), ())), preferred_element_type=F32)


def mm_nt(a, b):
    return lax.dot_general(a, b, (((1,), (1,)), ((), ())), preferred_element_type=F32)


def iota(shape, dim):
    return lax.broadcasted_iota(jnp.int32, shape, dim)


def greet(mode_peers, rad_peers):
    barrier = pltpu.get_barrier_semaphore()
    mode, rad = lax.axis_index("mode"), lax.axis_index("rad")
    if rad_peers:
        for d in range(1, RADS):
            pl.semaphore_signal(
                barrier, inc=1, device_id=(mode, lax.rem(rad + d, RADS)), device_id_type=MESH
            )
    if mode_peers:
        for d in range(1, MODES):
            pl.semaphore_signal(
                barrier, inc=1, device_id=(lax.rem(mode + d, MODES), rad), device_id_type=MESH
            )
    return barrier, (RADS - 1) * rad_peers + (MODES - 1) * mode_peers


def push_copy(src, dst, send, recv, mode, rad):
    return pltpu.make_async_remote_copy(
        src_ref=src,
        dst_ref=dst,
        send_sem=send,
        recv_sem=recv,
        device_id=(mode, rad),
        device_id_type=MESH,
    )


def radial_tiles(shape, dims):
    j = iota(shape, dims[0])
    sub = iota(shape, dims[1])
    return jnp.where(sub < 4, j, RADII - 1 - j), sub


def factor(mode, rad, diag_ref, edge_ref, g_ref):
    shape = (RADII // 2, 8, 128)
    r, sub = radial_tiles(shape, (0, 1))
    off = r.astype(F32)
    inverse = (RADII * RADII) / (off + 0.5)
    last = r == RADII - 1
    lower = off * inverse
    upper = jnp.where(last, 0.0, (off + 1.0) * inverse)
    centre = -(off + (off + 1.0) * jnp.where(last, 2.0, 1.0)) * inverse
    k = mode * KL + sub % KL
    kappa = 0.5 + 1.5 * k.astype(F32) / KZ
    coef = lax.rem(rad, 8) * 128 + iota(shape, 2)
    m = jnp.where(coef <= HALF, coef, coef - HALF).astype(F32)
    unit = (off + 0.5) / RADII
    diagonal = centre - m * m / (unit * unit) - kappa * kappa
    diag_ref[...] = 1.0 - implicit * diagonal
    top = sub < 4
    before = jnp.where(top, off - 1.0, off + 1.0)
    before_inverse = (RADII * RADII) / (before + 0.5)
    inward = jnp.where(top, (before + 1.0) * before_inverse, before * before_inverse)
    outward = jnp.where(top, lower, upper)
    edge_ref[...] = jnp.where(
        (r == 0) | last, 0.0, (implicit * implicit) * inward * outward
    )

    def step(j, g):
        g = 1.0 / (diag_ref[j] - edge_ref[j] * g)
        g_ref[j] = g
        return g

    lax.fori_loop(0, RADII // 2, step, jnp.zeros((8, 128), F32))


def dispatch(own, cell, pos, vel, rate, mass, fields_ref):
    owner = own[...]
    bands = iota((RADS, P_DEV), 0)
    match = (bands == owner).astype(F32)
    match_bf = match.astype(BF16)
    chunk = 256
    tri = (iota((chunk, chunk), 0) < iota((chunk, chunk), 1)).astype(F32).astype(BF16)
    running = jnp.zeros((RADS, 1), F32)
    places = []
    for n in range(P_DEV // chunk):
        part = match[:, n * chunk : (n + 1) * chunk]
        ahead = mm(match_bf[:, n * chunk : (n + 1) * chunk], tri) + running
        places.append(jnp.sum(ahead * part, axis=0, keepdims=True))
        running = running + jnp.sum(part, axis=1, keepdims=True)
    place = jnp.concatenate(places, axis=1).astype(jnp.int32)
    slots = (iota((CAP, P_DEV), 0) == place).astype(F32).astype(BF16)
    cells = cell[...]
    pieces = [(cells // ARC).astype(F32), (cells % ARC).astype(F32)]
    for ref in (pos, vel, rate, mass):
        left = ref[...]
        for _ in range(3):
            piece = left.astype(BF16).astype(F32)
            pieces.append(piece)
            left = left - piece
    rows = jnp.concatenate([jnp.where(match > 0.5, p, 0.0) for p in pieces], axis=0).astype(BF16)
    sorted_rows = mm_nt(rows, slots)

    def take(n):
        return sorted_rows[n * RADS : (n + 1) * RADS]

    fields_ref[:, 0, :] = take(0) * ARC + take(1)
    for f in range(4):
        fields_ref[:, 1 + f, :] = take(2 + 3 * f) + take(3 + 3 * f) + take(4 + 3 * f)
    for f in range(5, 8):
        fields_ref[:, f, :] = jnp.zeros((RADS, CAP), F32)


def cell_parts(cells):
    r = jnp.floor(cells * (1.0 / ARC))
    half = jnp.where(r >= BAND // 2, 1.0, 0.0)
    return cells + (half - r) * ARC, r - half * (BAND // 2)


QUARTER_HI = 1.57077026367187500
QUARTER_LO = math.pi / 2 - QUARTER_HI


def axial_tile(mode, positions):
    sub = iota((8, 1), 0)
    k = mode * KL + sub % KL
    kappa = 0.5 + 1.5 * k.astype(F32) / KZ
    phases = kappa * positions
    turns = jnp.floor(phases * (2.0 / math.pi) + 0.5)
    x = (phases - turns * QUARTER_HI) - turns * QUARTER_LO
    y = x * x
    sine = x + x * y * (-1.0 / 6 + y * (1.0 / 120 + y * (-1.0 / 5040 + y * (1.0 / 362880))))
    cosine = 1.0 + y * (-0.5 + y * (1.0 / 24 + y * (-1.0 / 720 + y * (1.0 / 40320))))
    quadrant = turns.astype(jnp.int32) + sub // KL
    scaling = 1.0 / math.sqrt(KZ)
    value = jnp.where((quadrant & 1) == 0, cosine, sine)
    return value * jnp.where(((quadrant + 1) & 2) == 0, scaling, -scaling)


HB = BAND // 2


def known_side(mode, rad, field, prior, known):
    lower, upper, centre, radius_sq = band_rows()
    coef = lax.rem(rad, 8) * 128 + iota((128, 1), 0)
    m_col = jnp.where(coef <= HALF, coef, coef - HALF).astype(F32)
    wave = m_col * m_col / radius_sq
    for k in range(KL):
        kappa = 0.5 + 1.5 * (mode * KL + k).astype(F32) / KZ
        f = field[k]
        diagonal = centre - wave - kappa * kappa
        laplace = lower * pltpu.roll(f, 1, 1) + diagonal * f + upper * pltpu.roll(f, RADII - 1, 1)
        side = f + time_step * (alpha_rk * viscosity * laplace + zeta_rk * prior[k])
        known[pl.ds(k, RADII, stride=KL), :] = jnp.transpose(side)


def forward(pieces, table_hi, table_lo, grid):
    sign = jnp.where(iota((1, AZIM), 1) % 2 == 0, 1.0, -1.0)
    xs = []
    for c in range(2):
        xs.append(jnp.concatenate(
            [pieces[(c * 8 + ib) * ROWS : (c * 8 + ib + 1) * ROWS, :] for ib in range(8)], axis=1
        ).reshape(HB, 8, AZIM))
    top = iota((1, 8, 1), 1) < KL
    even = jnp.where(top, xs[0], pltpu.roll(xs[1], 4, 1))
    odd = jnp.where(top, pltpu.roll(xs[0], 4, 1), xs[1])
    x = jnp.stack([even, odd], axis=1).reshape(2 * ROWS, AZIM)
    hi, lo = split(jnp.concatenate([x, x * sign], axis=0))
    for n in range(2):
        cols = slice(n * 256, (n + 1) * 256)
        th, tl = table_hi[:, cols], table_lo[:, cols]
        out = mm(hi, th) + mm(lo, th) + mm(hi, tl)
        for half in range(2):
            for a in range(2):
                grid[half * 4 + n * 2 + a] = out[
                    half * 2 * ROWS : (half + 1) * 2 * ROWS, a * 128 : (a + 1) * 128
                ]


def sample_arc(m, grid, gathered, onehots, weights, partial):
    hi, lo = split(jnp.concatenate([grid[m, :ROWS, :], grid[m, ROWS:, :]], axis=1))
    lhs = jnp.concatenate([hi, lo], axis=0)
    for s in range(RADS):
        _, rh = cell_parts(gathered[m, s : s + 1, :])
        both = mm(lhs, onehots[m, :, s * CAP : (s + 1) * CAP])
        values = both[:ROWS] + both[ROWS:]
        taken = jnp.zeros((8, CAP), F32)
        for q in range(HB):
            taken = jnp.where(rh == q, values[q * 8 : (q + 1) * 8], taken)
        partial[m, s : s + 1, :] = jnp.sum(taken * weights[m, s], axis=0, keepdims=True)


def deposit_arc(m, mode, grid, gathered, onehots, weights, pushes, flow, masses, terms):
    for s in range(RADS):
        _, rh = cell_parts(gathered[m, s : s + 1, :])
        value = pushes[m, s : s + 1, :] * weights[m, s]
        high = value.astype(BF16).astype(F32)
        low = value - high
        rows = [jnp.where(rh == q, high, 0.0) for q in range(HB)]
        rows += [jnp.where(rh == q, low, 0.0) for q in range(HB)]
        masses[:, s * CAP : (s + 1) * CAP] = jnp.concatenate(rows, axis=0).astype(BF16)
    both = mm_nt(masses[...], onehots[m])
    deposit = both[:ROWS] + both[ROWS:]
    sub = iota((8, 1), 0)
    kappa = 0.5 + 1.5 * (mode * KL + sub % KL).astype(F32) / KZ
    kappa = jnp.where(sub < KL, kappa, -kappa)
    for r in range(BAND):
        h, q = divmod(r, HB)
        rows = slice(r * 8, (r + 1) * 8)
        swapped = pltpu.roll(grid[m, rows, :], 4, 0)
        terms[m, rows, :] = (
            kappa * flow[m, r : r + 1, :] * swapped
            + deposit[q * 8 : (q + 1) * 8, h * 128 : (h + 1) * 128]
        )


def substep_body(
    field, prior, base, own, cell, pos, vel, rate, mass, table_hi, table_lo,
    returned, known, g_ref,
    outgoing, pieces, fields, arrived, gathered, diag, edge, flow, grid, terms, spectral,
    onehots, weights, masses, partial, parts, pushes,
    fsend, frecv, psend, precv, gsend, grecv, rsend, rrecv, asend, arecv, bsend, brecv,
):
    mode, rad = lax.axis_index("mode"), lax.axis_index("rad")
    barrier, count = greet(True, True)

    def rows(n):
        return pl.ds(pl.multiple_of(n * ROWS, 8), ROWS)

    def rad_peer(d):
        return lax.rem(rad + d, RADS)

    def mode_peer(d):
        return lax.rem(mode + d, MODES)

    def particle_copy(d):
        return push_copy(
            fields.at[rad_peer(d)], arrived.at[rad], psend.at[d], precv.at[d], mode, rad_peer(d)
        )

    def field_copy(d):
        return push_copy(
            outgoing.at[rows(rad_peer(d))], pieces.at[rows(rad)],
            fsend.at[d], frecv.at[d], mode, rad_peer(d),
        )

    def gather_copy(d):
        return push_copy(
            gathered.at[mode], gathered.at[mode], gsend.at[d], grecv.at[d], mode_peer(d), rad
        )

    def reduce_copy(d):
        return push_copy(
            partial.at[mode_peer(d)], parts.at[mode], rsend.at[d], rrecv.at[d], mode_peer(d), rad
        )

    def push_back(d):
        return push_copy(
            pushes.at[mode], pushes.at[mode], asend.at[d], arecv.at[d], mode_peer(d), rad
        )

    def back_copy(d):
        return push_copy(
            spectral.at[rows(rad_peer(d))], returned.at[rows(rad)],
            bsend.at[d], brecv.at[d], mode, rad_peer(d),
        )

    dispatch(own, cell, pos, vel, rate, mass, fields)
    pl.semaphore_wait(barrier, count)
    for d in range(1, RADS):
        particle_copy(d).start()
    for k in range(KL):
        outgoing[pl.ds(k, RADII, stride=KL), :] = jnp.transpose(field[k])
    for d in range(1, RADS):
        field_copy(d).start()
    arrived[rad] = fields[rad]
    pieces[rows(rad), :] = outgoing[rows(rad), :]
    for d in range(1, RADS):
        particle_copy(d).wait_recv()
    gathered[mode, 0:RADS, :] = arrived[:, 0, :]
    gathered[mode, RADS : 2 * RADS, :] = arrived[:, 1, :]
    for d in range(1, MODES):
        gather_copy(d).start()
    factor(mode, rad, diag, edge, g_ref)
    known_side(mode, rad, field, prior, known)
    for a in range(MODES):
        flow[a] = base[:, a * ARC : (a + 1) * ARC]
    for d in range(1, MODES):
        gather_copy(d).wait_recv()

    def prepare(m, carry):
        for s in range(RADS):
            column, _ = cell_parts(gathered[m, s : s + 1, :])
            index = iota((256, CAP), 0).astype(F32).astype(BF16)
            onehots[m, :, s * CAP : (s + 1) * CAP] = jnp.where(
                index == column.astype(BF16), jnp.ones((), BF16), jnp.zeros((), BF16)
            )
            weights[m, s] = axial_tile(mode, gathered[m, RADS + s : RADS + s + 1, :])
        return carry

    lax.fori_loop(0, MODES, prepare, 0)
    for d in range(1, RADS):
        field_copy(d).wait_recv()
    forward(pieces, table_hi, table_lo, grid)

    def sample(d, carry):
        sample_arc(mode_peer(d), grid, gathered, onehots, weights, partial)
        reduce_copy(d).start()
        return carry

    lax.fori_loop(1, MODES, sample, 0)
    sample_arc(mode, grid, gathered, onehots, weights, partial)
    parts[mode] = partial[mode]
    for d in range(1, MODES):
        reduce_copy(d).wait_recv()
    fluid = parts[0]
    for n in range(1, MODES):
        fluid = fluid + parts[n]
    relative = (fluid - arrived[:, 2, :]) * arrived[:, 3, :]
    pushes[mode] = -arrived[:, 4, :] * relative
    for d in range(1, MODES):
        push_back(d).start()

    def place(d, carry):
        @pl.when(d > 0)
        def _():
            push_back(MODES - d).wait_recv()

        deposit_arc(
            mode_peer(d), mode, grid, gathered, onehots, weights, pushes, flow, masses, terms
        )
        return carry

    lax.fori_loop(0, MODES, place, 0)
    first = jnp.concatenate([terms[a] for a in range(4)], axis=1)
    second = jnp.concatenate([terms[a + 4] for a in range(4)], axis=1)
    hi, lo = split(jnp.concatenate([first + second, first - second], axis=0))
    parity = iota((1, 128), 1) % 2 == 0
    top = iota((1, 8, 1), 1) < KL
    for ib in (0, 1, 2, 4, 5, 6):
        th, tl = table_hi[ib * 128 : (ib + 1) * 128, :], table_lo[ib * 128 : (ib + 1) * 128, :]
        out = mm_nt(hi, th) + mm_nt(lo, th) + mm_nt(hi, tl)
        chosen = jnp.where(parity, out[: 2 * ROWS], out[2 * ROWS :]).reshape(HB, 2, 8, 128)
        even, odd = chosen[:, 0], chosen[:, 1]
        real = jnp.where(top, even, pltpu.roll(odd, 4, 1))
        imag = jnp.where(top, pltpu.roll(even, 4, 1), odd)
        spectral[ib * ROWS : (ib + 1) * ROWS, :] = real.reshape(ROWS, 128)
        spectral[(8 + ib) * ROWS : (9 + ib) * ROWS, :] = imag.reshape(ROWS, 128)
    takes = lax.rem(rad, 4) != 3
    for d in range(1, RADS):
        @pl.when(lax.rem(rad_peer(d), 4) != 3)
        def _():
            back_copy(d).start()

    @pl.when(takes)
    def _():
        returned[rows(rad), :] = spectral[rows(rad), :]

    @pl.when(jnp.logical_not(takes))
    def _():
        returned[...] = jnp.zeros_like(returned)

    for d in range(1, RADS):
        particle_copy(d).wait_send()
        field_copy(d).wait_send()
    for d in range(1, MODES):
        gather_copy(d).wait_send()
        reduce_copy(d).wait_send()
        push_back(d).wait_send()
    for d in range(1, RADS):
        @pl.when(lax.rem(rad_peer(d), 4) != 3)
        def _():
            back_copy(d).wait_send()

        @pl.when(takes)
        def _():
            back_copy(d).wait_recv()


def band_rows():
    off = iota((1, RADII), 1).astype(F32)
    inverse = (RADII * RADII) / (off + 0.5)
    last = off == RADII - 1
    lower = off * inverse
    upper = jnp.where(last, 0.0, (off + 1.0) * inverse)
    centre = -(off + (off + 1.0) * jnp.where(last, 2.0, 1.0)) * inverse
    radius = (off + 0.5) / RADII
    return lower, upper, centre, radius * radius


def solve_body(returned, known, keep, g_ref, nxt, forcing, rhs, work):
    rad = lax.axis_index("rad")
    half = RADII // 2
    lane = lax.rem(rad, 8) * 128 + iota((8, 128), 1)
    m = jnp.where(lane <= HALF, lane, lane - HALF)
    sub = iota((8, 128), 0)
    most = jnp.where(
        sub % KL == 0, keep[0], jnp.where(sub % KL == 1, keep[1], jnp.where(sub % KL == 2, keep[2], keep[3]))
    )
    kept_here = m <= most
    top = sub < KL
    gain = time_step * gamma_rk

    def rows(q):
        return pl.ds(pl.multiple_of(q * 8, 8), 8)

    def fold(q, carry):
        sides = []
        for n in (q, half - 1 - q):
            kept = jnp.where(kept_here, returned[rows(n), :], 0.0)
            rhs[rows(n), :] = kept
            sides.append(known[rows(n), :] + gain * kept)
        work[2 * q] = jnp.where(top, sides[0], sides[1]) * g_ref[2 * q]
        odd = pltpu.roll(jnp.where(top, sides[1], sides[0]), 4, 0)
        work[2 * q + 1] = odd * g_ref[2 * q + 1]
        return carry

    lax.fori_loop(0, half // 2, fold, 0, unroll=8)
    for k in range(KL):
        forcing[k] = jnp.transpose(rhs[pl.ds(k, RADII, stride=KL), :])

    scale = -implicit * RADII * RADII

    def couplings(j):
        r = jnp.where(top, j, RADII - 1 - j)
        off = r.astype(F32)
        inverse = scale / (off + 0.5)
        after = jnp.where(r == RADII - 1, 0.0, off + 1.0)
        return jnp.where(top, off, after) * inverse, jnp.where(top, after, off) * inverse

    def down(j, d):
        outer, _ = couplings(j)
        d = work[j] - (outer * g_ref[j]) * d
        work[j] = d
        return d

    d = lax.fori_loop(0, half, down, jnp.zeros((8, 128), F32), unroll=8)
    _, inner = couplings(half - 1)
    v = inner * g_ref[half - 1]
    x = (d - v * pltpu.roll(d, 4, 0)) / (1.0 - v * pltpu.roll(v, 4, 0))
    work[half - 1] = x

    def back(n, x):
        j = half - 2 - n
        _, inner = couplings(j)
        x = work[j] - (inner * g_ref[j]) * x
        work[j] = x
        return x

    lax.fori_loop(0, half - 1, back, x, unroll=8)

    def unfold(q, carry):
        even = work[2 * q]
        odd = pltpu.roll(work[2 * q + 1], 4, 0)
        rhs[rows(q), :] = jnp.where(top, even, odd)
        rhs[rows(half - 1 - q), :] = jnp.where(top, odd, even)
        return carry

    lax.fori_loop(0, half // 2, unfold, 0, unroll=8)
    for k in range(KL):
        nxt[k] = jnp.transpose(rhs[pl.ds(k, RADII, stride=KL), :])


def vmem_call(body, outs, n_in, scratch, collective=None, smem=(), name=None):
    spec = [
        pl.BlockSpec(memory_space=pltpu.SMEM if n in smem else VMEM) for n in range(n_in)
    ]
    params = dict(vmem_limit_bytes=56 * 1024 * 1024)
    if collective is not None:
        params.update(collective_id=collective, has_side_effects=True)
    return pl.pallas_call(
        body,
        out_shape=[jax.ShapeDtypeStruct(s, F32) for s in outs],
        in_specs=spec,
        out_specs=[pl.BlockSpec(memory_space=VMEM)] * len(outs),
        scratch_shapes=scratch,
        compiler_params=pltpu.CompilerParams(**params),
        name=name,
    )


DMA = pltpu.SemaphoreType.DMA


def per_device(
    field_coef,
    prior_forcing,
    base_flow,
    keep_modes,
    owner_band,
    cell_index,
    axial_pos,
    particle_vel,
    response_rate,
    particle_mass,
):
    high, low = fourier_half()
    table_hi, table_lo = jnp.asarray(high), jnp.asarray(low)

    def row(x):
        return x.reshape(1, P_DEV)

    all_rows = (RADS * ROWS, 128)
    tiles = (RADII // 2, 8, 128)
    slots = (MODES, RADS, CAP)
    returned, known, g = vmem_call(
        substep_body,
        [all_rows, all_rows, tiles],
        11,
        [
            VMEM(all_rows, F32),
            VMEM(all_rows, F32),
            VMEM((RADS, 8, CAP), F32),
            VMEM((RADS, 8, CAP), F32),
            VMEM((MODES, 2 * RADS, CAP), F32),
            VMEM(tiles, F32),
            VMEM(tiles, F32),
            VMEM((MODES, BAND, ARC), F32),
            VMEM((MODES, 2 * ROWS, 128), F32),
            VMEM((MODES, 2 * ROWS, 128), F32),
            VMEM(all_rows, F32),
            VMEM((MODES, 256, RADS * CAP), BF16),
            VMEM((MODES, RADS, 8, CAP), F32),
            VMEM((2 * ROWS, RADS * CAP), BF16),
            VMEM(slots, F32),
            VMEM(slots, F32),
            VMEM(slots, F32),
            DMA((RADS,)), DMA((RADS,)), DMA((RADS,)), DMA((RADS,)),
            DMA((MODES,)), DMA((MODES,)), DMA((MODES,)), DMA((MODES,)),
            DMA((MODES,)), DMA((MODES,)), DMA((RADS,)), DMA((RADS,)),
        ],
        collective=0,
        name="substep",
    )(
        field_coef, prior_forcing, base_flow, row(owner_band), row(cell_index), row(axial_pos),
        row(particle_vel), row(response_rate), row(particle_mass), table_hi, table_lo,
    )
    field_next, forcing = vmem_call(
        solve_body,
        [(KL, 128, RADII), (KL, 128, RADII)],
        4,
        [VMEM(all_rows, F32), VMEM(tiles, F32)],
        smem=(2,),
        name="solve",
    )(returned, known, keep_modes, g)
    return (field_next, forcing)


def solution(mesh):
    in_specs = (
        P("mode", "rad", None),
        P("mode", "rad", None),
        P("rad", None),
        P("mode"),
        P(("mode", "rad"), None),
        P(("mode", "rad")),
        P(("mode", "rad")),
        P(("mode", "rad")),
        P(("mode", "rad")),
        P(("mode", "rad")),
    )
    out_specs = (P("mode", "rad", None), P("mode", "rad", None))
    return jax.shard_map(
        per_device, mesh=mesh, in_specs=in_specs, out_specs=out_specs, check_vma=False
    )
```

time: 94.1 us -> 66.1 us (0.70)
  the two profiles are of different devices: /device:TPU:1 before, /device:TPU:17 now
where the time goes in v1:
time: 66.1 us; the launch traced here: 65.9 us
  Pallas kernels  65.3 us (99%)
    pallas_call x1, Pallas kernels, per_device(): vmem_call(substep_body, [all_rows, all_rows, tiles], 11, [VMEM(all_rows,...  60.2 us
    pallas_call x1, Pallas kernels, per_device(): vmem_call(solve_body, [(KL, 128, RADII), (KL, 128, RADII)], 4, [VMEM(all_...  5.12 us

profile of v1, /device:TPU:17, one launch (start us, length us, event | category | flops | bytes accessed | tf_op | source)
XLA Modules:
  0.0 65.9 jit_solution(3365929514331318063)
XLA Ops:
  0.6 60.2 %substep.1 = (f32[1536,128]{1,0:T(8,128)}, f32[1536,128]{1,0:T(8,128)}, f32[192,8,128]{2,1,0:T(8,128)}) custom-call(f32[4,128,384]{2,1,0:T(8,128)} %field.1, f32[4,128,384]{2,1,0:T(8,128)} %prior.1, f32[24,1024]{1,0:T(8,128)} %base.1, s32[1,2048]{1,0:T(1,128)} %bitcast.6, s32[1,2048]{1,0:T(1,128)} %bitcast.7, f32[1,2048]{1,0:T(1,128)} %bitcast.8, ...), custom_call_target="tpu_custom_call" | custom-call | tf_op jit(solution)/shard_map/substep/pallas_call | solution.py:564
  60.8 5.1 %solve.1 = (f32[4,128,384]{2,1,0:T(8,128)}, f32[4,128,384]{2,1,0:T(8,128)}) custom-call(f32[1536,128]{1,0:T(8,128)} %get-tuple-element.5.returned, f32[1536,128]{1,0:T(8,128)} %get-tuple-element.6.known, s32[4]{0:T(128)} %keep.1, f32[192,8,128]{2,1,0:T(8,128)} %get-tuple-element.7.g_ref), custom_call_target="tpu_custom_call" | custom-call | tf_op jit(solution)/shard_map/solve/pallas_call | solution.py:596

commit v2 on v1

--- a/solution.py
+++ b/solution.py
@@ -196,6 +196,7 @@
 
 
 HB = BAND // 2
+EARLY = 0
 
 
 def known_side(mode, rad, field, prior, known):
@@ -248,7 +249,7 @@
         partial[m, s : s + 1, :] = jnp.sum(taken * weights[m, s], axis=0, keepdims=True)
 
 
-def deposit_arc(m, mode, grid, gathered, onehots, weights, pushes, flow, masses, terms):
+def deposit_arc(m, gathered, onehots, weights, pushes, masses, terms):
     for s in range(RADS):
         _, rh = cell_parts(gathered[m, s : s + 1, :])
         value = pushes[m, s : s + 1, :] * weights[m, s]
@@ -259,28 +260,39 @@
         masses[:, s * CAP : (s + 1) * CAP] = jnp.concatenate(rows, axis=0).astype(BF16)
     both = mm_nt(masses[...], onehots[m])
     deposit = both[:ROWS] + both[ROWS:]
+    for h in range(2):
+        rows = slice(h * ROWS, (h + 1) * ROWS)
+        terms[m, rows, :] = terms[m, rows, :] + deposit[:, h * 128 : (h + 1) * 128]
+
+
+def advect_arc(m, mode, grid, flow, terms):
     sub = iota((8, 1), 0)
     kappa = 0.5 + 1.5 * (mode * KL + sub % KL).astype(F32) / KZ
     kappa = jnp.where(sub < KL, kappa, -kappa)
     for r in range(BAND):
-        h, q = divmod(r, HB)
         rows = slice(r * 8, (r + 1) * 8)
         swapped = pltpu.roll(grid[m, rows, :], 4, 0)
-        terms[m, rows, :] = (
-            kappa * flow[m, r : r + 1, :] * swapped
-            + deposit[q * 8 : (q + 1) * 8, h * 128 : (h + 1) * 128]
-        )
+        terms[m, rows, :] = kappa * flow[m, r : r + 1, :] * swapped
 
 
 def substep_body(
-    field, prior, base, own, cell, pos, vel, rate, mass, table_hi, table_lo,
-    returned, known, g_ref,
+    field_in, prior_in, base_in, own_in, cell_in, pos_in, vel_in, rate_in, mass_in, hi_in, lo_in,
+    returned, known_out, g_out,
+    field, prior, base, own, cell, pos, vel, rate, mass, table_hi, table_lo, known, g_ref,
     outgoing, pieces, fields, arrived, gathered, diag, edge, flow, grid, terms, spectral,
-    onehots, weights, masses, partial, parts, pushes,
+    onehots, weights, masses, splits, partial, parts, pushes, loads, stores,
     fsend, frecv, psend, precv, gsend, grecv, rsend, rrecv, asend, arecv, bsend, brecv,
 ):
     mode, rad = lax.axis_index("mode"), lax.axis_index("rad")
     barrier, count = greet(True, True)
+    given = [
+        (own_in, own), (cell_in, cell), (pos_in, pos), (vel_in, vel), (rate_in, rate),
+        (mass_in, mass), (field_in, field), (hi_in, table_hi), (lo_in, table_lo),
+        (prior_in, prior), (base_in, base),
+    ]
+    given = [pltpu.make_async_copy(x, y, loads.at[n]) for n, (x, y) in enumerate(given)]
+    for copy in given:
+        copy.start()
 
     def rows(n):
         return pl.ds(pl.multiple_of(n * ROWS, 8), ROWS)
@@ -323,13 +335,16 @@
             bsend.at[d], brecv.at[d], mode, rad_peer(d),
         )
 
+    for copy in given[:6]:
+        copy.wait()
     dispatch(own, cell, pos, vel, rate, mass, fields)
     pl.semaphore_wait(barrier, count)
     for d in range(1, RADS):
         particle_copy(d).start()
+    given[6].wait()
     for k in range(KL):
         outgoing[pl.ds(k, RADII, stride=KL), :] = jnp.transpose(field[k])
-    for d in range(1, RADS):
+    for d in range(1, 1 + EARLY):
         field_copy(d).start()
     arrived[rad] = fields[rad]
     pieces[rows(rad), :] = outgoing[rows(rad), :]
@@ -337,16 +352,17 @@
         particle_copy(d).wait_recv()
     gathered[mode, 0:RADS, :] = arrived[:, 0, :]
     gathered[mode, RADS : 2 * RADS, :] = arrived[:, 1, :]
-    for d in range(1, MODES):
+    for d in (4, 3, 5, 2, 6, 1, 7):
         gather_copy(d).start()
-    factor(mode, rad, diag, edge, g_ref)
-    known_side(mode, rad, field, prior, known)
-    for a in range(MODES):
-        flow[a] = base[:, a * ARC : (a + 1) * ARC]
-    for d in range(1, MODES):
-        gather_copy(d).wait_recv()
-
-    def prepare(m, carry):
+    for d in range(1 + EARLY, RADS):
+        field_copy(d).start()
+
+    def prepare(d, carry):
+        @pl.when(d > 0)
+        def _():
+            gather_copy(MODES - d).wait_recv()
+
+        m = mode_peer(d)
         for s in range(RADS):
             column, _ = cell_parts(gathered[m, s : s + 1, :])
             index = iota((256, CAP), 0).astype(F32).astype(BF16)
@@ -356,19 +372,39 @@
             weights[m, s] = axial_tile(mode, gathered[m, RADS + s : RADS + s + 1, :])
         return carry
 
+    for copy in given[7:]:
+        copy.wait()
+    for a in range(MODES):
+        flow[a] = base[:, a * ARC : (a + 1) * ARC]
     lax.fori_loop(0, MODES, prepare, 0)
+    factor(mode, rad, diag, edge, g_ref)
+    known_side(mode, rad, field, prior, known)
+    kept = [
+        pltpu.make_async_copy(known, known_out, stores.at[0]),
+        pltpu.make_async_copy(g_ref, g_out, stores.at[1]),
+    ]
+    for copy in kept:
+        copy.start()
+
     for d in range(1, RADS):
         field_copy(d).wait_recv()
     forward(pieces, table_hi, table_lo, grid)
 
-    def sample(d, carry):
+    def sample(n, carry):
+        d = lax.rem(n + 2, 7) + 1
         sample_arc(mode_peer(d), grid, gathered, onehots, weights, partial)
         reduce_copy(d).start()
         return carry
 
-    lax.fori_loop(1, MODES, sample, 0)
+    lax.fori_loop(0, MODES - 1, sample, 0)
     sample_arc(mode, grid, gathered, onehots, weights, partial)
     parts[mode] = partial[mode]
+
+    def advect(m, carry):
+        advect_arc(m, mode, grid, flow, terms)
+        return carry
+
+    lax.fori_loop(0, MODES // 2, advect, 0)
     for d in range(1, MODES):
         reduce_copy(d).wait_recv()
     fluid = parts[0]
@@ -376,48 +412,58 @@
         fluid = fluid + parts[n]
     relative = (fluid - arrived[:, 2, :]) * arrived[:, 3, :]
     pushes[mode] = -arrived[:, 4, :] * relative
-    for d in range(1, MODES):
+    for d in (4, 3, 5, 2, 6, 1, 7):
         push_back(d).start()
-
-    def place(d, carry):
-        @pl.when(d > 0)
-        def _():
-            push_back(MODES - d).wait_recv()
-
-        deposit_arc(
-            mode_peer(d), mode, grid, gathered, onehots, weights, pushes, flow, masses, terms
-        )
+    lax.fori_loop(MODES // 2, MODES, advect, 0)
+    deposit_arc(mode, gathered, onehots, weights, pushes, masses, terms)
+
+    def place(n, carry):
+        d = lax.rem(n + 5, 7) + 1
+        push_back(MODES - d).wait_recv()
+        deposit_arc(mode_peer(d), gathered, onehots, weights, pushes, masses, terms)
         return carry
 
-    lax.fori_loop(0, MODES, place, 0)
+    lax.fori_loop(0, MODES - 1, place, 0)
     first = jnp.concatenate([terms[a] for a in range(4)], axis=1)
     second = jnp.concatenate([terms[a + 4] for a in range(4)], axis=1)
     hi, lo = split(jnp.concatenate([first + second, first - second], axis=0))
+    splits[0] = hi
+    splits[1] = lo
     parity = iota((1, 128), 1) % 2 == 0
     top = iota((1, 8, 1), 1) < KL
-    for ib in (0, 1, 2, 4, 5, 6):
-        th, tl = table_hi[ib * 128 : (ib + 1) * 128, :], table_lo[ib * 128 : (ib + 1) * 128, :]
-        out = mm_nt(hi, th) + mm_nt(lo, th) + mm_nt(hi, tl)
+
+    def inverse(n, carry):
+        j = lax.rem(rad + n, 6)
+        ib = j + j // 3
+        block = pl.ds(pl.multiple_of(ib * 128, 128), 128)
+        th, tl = table_hi[block, :], table_lo[block, :]
+        out = mm_nt(splits[0], th) + mm_nt(splits[1], th) + mm_nt(splits[0], tl)
         chosen = jnp.where(parity, out[: 2 * ROWS], out[2 * ROWS :]).reshape(HB, 2, 8, 128)
         even, odd = chosen[:, 0], chosen[:, 1]
         real = jnp.where(top, even, pltpu.roll(odd, 4, 1))
         imag = jnp.where(top, pltpu.roll(even, 4, 1), odd)
-        spectral[ib * ROWS : (ib + 1) * ROWS, :] = real.reshape(ROWS, 128)
-        spectral[(8 + ib) * ROWS : (9 + ib) * ROWS, :] = imag.reshape(ROWS, 128)
+        spectral[rows(ib), :] = real.reshape(ROWS, 128)
+        spectral[rows(8 + ib), :] = imag.reshape(ROWS, 128)
+        for c in range(2):
+            d = lax.rem(c * 8 + ib - rad + RADS, RADS)
+
+            @pl.when(d > 0)
+            def _():
+                back_copy(d).start()
+
+            @pl.when(d == 0)
+            def _():
+                own_back.start()
+
+        return carry
+
+    own_back = pltpu.make_async_copy(
+        spectral.at[rows(rad)], returned.at[rows(rad)], stores.at[2]
+    )
+    lax.fori_loop(0, 6, inverse, 0)
     takes = lax.rem(rad, 4) != 3
-    for d in range(1, RADS):
-        @pl.when(lax.rem(rad_peer(d), 4) != 3)
-        def _():
-            back_copy(d).start()
-
-    @pl.when(takes)
-    def _():
-        returned[rows(rad), :] = spectral[rows(rad), :]
-
-    @pl.when(jnp.logical_not(takes))
-    def _():
-        returned[...] = jnp.zeros_like(returned)
-
+    for copy in kept:
+        copy.wait()
     for d in range(1, RADS):
         particle_copy(d).wait_send()
         field_copy(d).wait_send()
@@ -434,6 +480,10 @@
         def _():
             back_copy(d).wait_recv()
 
+    @pl.when(takes)
+    def _():
+        own_back.wait()
+
 
 def band_rows():
     off = iota((1, RADII), 1).astype(F32)
@@ -519,9 +569,9 @@
         nxt[k] = jnp.transpose(rhs[pl.ds(k, RADII, stride=KL), :])
 
 
-def vmem_call(body, outs, n_in, scratch, collective=None, smem=(), name=None):
+def vmem_call(body, outs, n_in, scratch, collective=None, smem=(), name=None, space=VMEM):
     spec = [
-        pl.BlockSpec(memory_space=pltpu.SMEM if n in smem else VMEM) for n in range(n_in)
+        pl.BlockSpec(memory_space=pltpu.SMEM if n in smem else space) for n in range(n_in)
     ]
     params = dict(vmem_limit_bytes=56 * 1024 * 1024)
     if collective is not None:
@@ -530,7 +580,7 @@
         body,
         out_shape=[jax.ShapeDtypeStruct(s, F32) for s in outs],
         in_specs=spec,
-        out_specs=[pl.BlockSpec(memory_space=VMEM)] * len(outs),
+        out_specs=[pl.BlockSpec(memory_space=space)] * len(outs),
         scratch_shapes=scratch,
         compiler_params=pltpu.CompilerParams(**params),
         name=name,
@@ -566,6 +616,19 @@
         [all_rows, all_rows, tiles],
         11,
         [
+            VMEM(field_coef.shape, F32),
+            VMEM(field_coef.shape, F32),
+            VMEM(base_flow.shape, F32),
+            VMEM((1, P_DEV), jnp.int32),
+            VMEM((1, P_DEV), jnp.int32),
+            VMEM((1, P_DEV), F32),
+            VMEM((1, P_DEV), F32),
+            VMEM((1, P_DEV), F32),
+            VMEM((1, P_DEV), F32),
+            VMEM(table_hi.shape, BF16),
+            VMEM(table_hi.shape, BF16),
+            VMEM(all_rows, F32),
+            VMEM(tiles, F32),
             VMEM(all_rows, F32),
             VMEM(all_rows, F32),
             VMEM((RADS, 8, CAP), F32),
@@ -580,15 +643,18 @@
             VMEM((MODES, 256, RADS * CAP), BF16),
             VMEM((MODES, RADS, 8, CAP), F32),
             VMEM((2 * ROWS, RADS * CAP), BF16),
+            VMEM((2, 4 * ROWS, HALF), BF16),
             VMEM(slots, F32),
             VMEM(slots, F32),
             VMEM(slots, F32),
+            DMA((11,)), DMA((3,)),
             DMA((RADS,)), DMA((RADS,)), DMA((RADS,)), DMA((RADS,)),
             DMA((MODES,)), DMA((MODES,)), DMA((MODES,)), DMA((MODES,)),
             DMA((MODES,)), DMA((MODES,)), DMA((RADS,)), DMA((RADS,)),
         ],
         collective=0,
         name="substep",
+        space=pl.ANY,
     )(
         field_coef, prior_forcing, base_flow, row(owner_band), row(cell_index), row(axial_pos),
         row(particle_vel), row(response_rate), row(particle_mass), table_hi, table_lo,

time: 66.1 us -> 60.9 us (0.921)
  the two profiles are of different devices: /device:TPU:17 before, /device:TPU:1 now
where the time goes in v2:
time: 60.9 us; the launch traced here: 60.1 us
  Pallas kernels  59.4 us (98%)
  between operations  0.64 us (1%)
    pallas_call x1, Pallas kernels, per_device(): vmem_call(substep_body, [all_rows, all_rows, tiles], 11, [VMEM(field_coef...  54.3 us
    pallas_call x1, Pallas kernels, per_device(): vmem_call(solve_body, [(KL, 128, RADII), (KL, 128, RADII)], 4, [VMEM(all_...  5.12 us

profile of v2, /device:TPU:1, one launch (start us, length us, event | category | flops | bytes accessed | tf_op | source)
XLA Modules:
  0.0 60.1 jit_solution(7014920956714814202)
XLA Ops:
  0.6 54.3 %substep.1 = (f32[1536,128]{1,0:T(8,128)}, f32[1536,128]{1,0:T(8,128)}, f32[192,8,128]{2,1,0:T(8,128)}) custom-call(f32[4,128,384]{2,1,0:T(8,128)} %field_in.1, f32[4,128,384]{2,1,0:T(8,128)} %prior_in.1, f32[24,1024]{1,0:T(8,128)} %base_in.1, s32[1,2048]{1,0:T(1,128)} %bitcast.6, s32[1,2048]{1,0:T(1,128)} %bitcast.7, f32[1,2048]{1,0:T(1,128)} %bitcast.8, ...), custom_call_target="tpu_custom_call" | custom-call | tf_op jit(solution)/shard_map/substep/pallas_call | solution.py:614
  55.0 5.1 %solve.1 = (f32[4,128,384]{2,1,0:T(8,128)}, f32[4,128,384]{2,1,0:T(8,128)}) custom-call(f32[1536,128]{1,0:T(8,128)} %get-tuple-element.5.returned, f32[1536,128]{1,0:T(8,128)} %get-tuple-element.6.known, s32[4]{0:T(128)} %keep.1, f32[192,8,128]{2,1,0:T(8,128)} %get-tuple-element.7.g_ref), custom_call_target="tpu_custom_call" | custom-call | tf_op jit(solution)/shard_map/solve/pallas_call | solution.py:662

commit v3 on v2

--- a/solution.py
+++ b/solution.py
@@ -105,8 +105,6 @@
     off = r.astype(F32)
     inverse = (RADII * RADII) / (off + 0.5)
     last = r == RADII - 1
-    lower = off * inverse
-    upper = jnp.where(last, 0.0, (off + 1.0) * inverse)
     centre = -(off + (off + 1.0) * jnp.where(last, 2.0, 1.0)) * inverse
     k = mode * KL + sub % KL
     kappa = 0.5 + 1.5 * k.astype(F32) / KZ
@@ -114,15 +112,9 @@
     m = jnp.where(coef <= HALF, coef, coef - HALF).astype(F32)
     unit = (off + 0.5) / RADII
     diagonal = centre - m * m / (unit * unit) - kappa * kappa
-    diag_ref[...] = 1.0 - implicit * diagonal
-    top = sub < 4
-    before = jnp.where(top, off - 1.0, off + 1.0)
-    before_inverse = (RADII * RADII) / (before + 0.5)
-    inward = jnp.where(top, (before + 1.0) * before_inverse, before * before_inverse)
-    outward = jnp.where(top, lower, upper)
-    edge_ref[...] = jnp.where(
-        (r == 0) | last, 0.0, (implicit * implicit) * inward * outward
-    )
+    diag_ref[...] = (1.0 - implicit * diagonal) * (off + 0.5)
+    outer = (implicit * RADII * RADII) * jnp.where(sub < 4, off, off + 1.0)
+    edge_ref[...] = outer * outer
 
     def step(j, g):
         g = 1.0 / (diag_ref[j] - edge_ref[j] * g)
@@ -196,7 +188,8 @@
 
 
 HB = BAND // 2
-EARLY = 0
+EARLY = 10
+NEAR = (1, 3, 4, 12, 2, 5, 7, 8, 13, 15, 6, 14, 9, 11, 10)
 
 
 def known_side(mode, rad, field, prior, known):
@@ -280,8 +273,9 @@
     returned, known_out, g_out,
     field, prior, base, own, cell, pos, vel, rate, mass, table_hi, table_lo, known, g_ref,
     outgoing, pieces, fields, arrived, gathered, diag, edge, flow, grid, terms, spectral,
-    onehots, weights, masses, splits, partial, parts, pushes, loads, stores,
-    fsend, frecv, psend, precv, gsend, grecv, rsend, rrecv, asend, arecv, bsend, brecv,
+    onehots, weights, masses, splits, partial, twins, totals, parts, pushes, loads, stores,
+    fsend, frecv, psend, precv, gsend, grecv, tsend, trecv, rsend, rrecv, asend, arecv, csend, crecv,
+    bsend, brecv,
 ):
     mode, rad = lax.axis_index("mode"), lax.axis_index("rad")
     barrier, count = greet(True, True)
@@ -297,8 +291,12 @@
     def rows(n):
         return pl.ds(pl.multiple_of(n * ROWS, 8), ROWS)
 
+    x, y = rad // 4, lax.rem(rad, 4)
+    z, core = mode // 2, lax.rem(mode, 2)
+    twin = z * 2 + 1 - core
+
     def rad_peer(d):
-        return lax.rem(rad + d, RADS)
+        return lax.rem(x + d // 4, 4) * 4 + lax.rem(y + lax.rem(d, 4), 4)
 
     def mode_peer(d):
         return lax.rem(mode + d, MODES)
@@ -319,14 +317,29 @@
             gathered.at[mode], gathered.at[mode], gsend.at[d], grecv.at[d], mode_peer(d), rad
         )
 
-    def reduce_copy(d):
+    def above(o):
+        return lax.rem(z + o, 4) * 2 + core
+
+    def twin_part(o):
         return push_copy(
-            partial.at[mode_peer(d)], parts.at[mode], rsend.at[d], rrecv.at[d], mode_peer(d), rad
+            partial.at[lax.rem(z + o, 4) * 2 + 1 - core], twins.at[o],
+            tsend.at[o], trecv.at[o], twin, rad,
         )
 
-    def push_back(d):
+    def reduce_copy(o):
         return push_copy(
-            pushes.at[mode], pushes.at[mode], asend.at[d], arecv.at[d], mode_peer(d), rad
+            totals.at[o], parts.at[o], rsend.at[o], rrecv.at[o], above(o), rad
+        )
+
+    def push_copy_above(o):
+        return push_copy(
+            pushes.at[mode], pushes.at[mode], asend.at[o], arecv.at[o], above(o), rad
+        )
+
+    def push_copy_twin(o):
+        from_below = lax.rem(z - o + 4, 4) * 2 + core
+        return push_copy(
+            pushes.at[from_below], pushes.at[from_below], csend.at[o], crecv.at[o], twin, rad
         )
 
     def back_copy(d):
@@ -338,24 +351,36 @@
     for copy in given[:6]:
         copy.wait()
     dispatch(own, cell, pos, vel, rate, mass, fields)
-    pl.semaphore_wait(barrier, count)
-    for d in range(1, RADS):
-        particle_copy(d).start()
     given[6].wait()
     for k in range(KL):
         outgoing[pl.ds(k, RADII, stride=KL), :] = jnp.transpose(field[k])
-    for d in range(1, 1 + EARLY):
+    pl.semaphore_wait(barrier, count)
+    for d in NEAR[::-1]:
+        particle_copy(d).start()
+    for d in NEAR[:EARLY]:
         field_copy(d).start()
     arrived[rad] = fields[rad]
     pieces[rows(rad), :] = outgoing[rows(rad), :]
-    for d in range(1, RADS):
+    for copy in given[7:]:
+        copy.wait()
+    known_side(mode, rad, field, prior, known)
+    for d in NEAR:
         particle_copy(d).wait_recv()
     gathered[mode, 0:RADS, :] = arrived[:, 0, :]
     gathered[mode, RADS : 2 * RADS, :] = arrived[:, 1, :]
     for d in (4, 3, 5, 2, 6, 1, 7):
         gather_copy(d).start()
-    for d in range(1 + EARLY, RADS):
+    for d in NEAR[EARLY:]:
         field_copy(d).start()
+    factor(mode, rad, diag, edge, g_ref)
+    kept = [
+        pltpu.make_async_copy(known, known_out, stores.at[0]),
+        pltpu.make_async_copy(g_ref, g_out, stores.at[1]),
+    ]
+    for copy in kept:
+        copy.start()
+    for a in range(MODES):
+        flow[a] = base[:, a * ARC : (a + 1) * ARC]
 
     def prepare(d, carry):
         @pl.when(d > 0)
@@ -372,58 +397,78 @@
             weights[m, s] = axial_tile(mode, gathered[m, RADS + s : RADS + s + 1, :])
         return carry
 
-    for copy in given[7:]:
-        copy.wait()
-    for a in range(MODES):
-        flow[a] = base[:, a * ARC : (a + 1) * ARC]
     lax.fori_loop(0, MODES, prepare, 0)
-    factor(mode, rad, diag, edge, g_ref)
-    known_side(mode, rad, field, prior, known)
-    kept = [
-        pltpu.make_async_copy(known, known_out, stores.at[0]),
-        pltpu.make_async_copy(g_ref, g_out, stores.at[1]),
-    ]
-    for copy in kept:
-        copy.start()
-
     for d in range(1, RADS):
         field_copy(d).wait_recv()
     forward(pieces, table_hi, table_lo, grid)
 
-    def sample(n, carry):
-        d = lax.rem(n + 2, 7) + 1
-        sample_arc(mode_peer(d), grid, gathered, onehots, weights, partial)
-        reduce_copy(d).start()
+    def outward(n):
+        t = lax.rem(n + 2, 4)
+        return t + (n // 2) * (1 - 2 * t)
+
+    def sample_twin(n, carry):
+        o = outward(n)
+        m = lax.rem(z + o, 4) * 2 + 1 - core
+        sample_arc(m, grid, gathered, onehots, weights, partial)
+        twin_part(o).start()
         return carry
 
-    lax.fori_loop(0, MODES - 1, sample, 0)
-    sample_arc(mode, grid, gathered, onehots, weights, partial)
-    parts[mode] = partial[mode]
+    def sample_own(n, carry):
+        o = outward(n)
+        m = above(o)
+        sample_arc(m, grid, gathered, onehots, weights, partial)
+        twin_part(o).wait_recv()
+        totals[o] = partial[m] + twins[o]
+
+        @pl.when(o > 0)
+        def _():
+            reduce_copy(o).start()
+
+        return carry
 
     def advect(m, carry):
         advect_arc(m, mode, grid, flow, terms)
         return carry
 
-    lax.fori_loop(0, MODES // 2, advect, 0)
-    for d in range(1, MODES):
-        reduce_copy(d).wait_recv()
-    fluid = parts[0]
-    for n in range(1, MODES):
-        fluid = fluid + parts[n]
+    lax.fori_loop(0, 4, sample_twin, 0)
+    lax.fori_loop(0, 4, sample_own, 0)
+    lax.fori_loop(0, MODES, advect, 0)
+    for o in (1, 3, 2):
+        reduce_copy(o).wait_recv()
+    fluid = (totals[0] + parts[1]) + (parts[2] + parts[3])
     relative = (fluid - arrived[:, 2, :]) * arrived[:, 3, :]
     pushes[mode] = -arrived[:, 4, :] * relative
-    for d in (4, 3, 5, 2, 6, 1, 7):
-        push_back(d).start()
-    lax.fori_loop(MODES // 2, MODES, advect, 0)
-    deposit_arc(mode, gathered, onehots, weights, pushes, masses, terms)
+    for o in (2, 3, 1):
+        push_copy_above(o).start()
+    push_copy_twin(0).start()
+
+    def arrive(o):
+        push_copy_above(o).wait_recv()
+        push_copy_twin(o).start()
 
     def place(n, carry):
-        d = lax.rem(n + 5, 7) + 1
-        push_back(MODES - d).wait_recv()
-        deposit_arc(mode_peer(d), gathered, onehots, weights, pushes, masses, terms)
+        j = jnp.where(n < 2, 0, lax.rem(n - 2, 3) + 1)
+        o = j + (j // 2) * (5 - 2 * j)
+        b = jnp.where((n == 1) | (n > 4), 1, 0)
+
+        @pl.when(n == 2)
+        def _():
+            arrive(1)
+            arrive(3)
+
+        @pl.when(n == 3)
+        def _():
+            arrive(2)
+
+        @pl.when(b == 1)
+        def _():
+            push_copy_twin(o).wait_recv()
+
+        m = lax.rem(z - o + 4, 4) * 2 + lax.rem(core + b, 2)
+        deposit_arc(m, gathered, onehots, weights, pushes, masses, terms)
         return carry
 
-    lax.fori_loop(0, MODES - 1, place, 0)
+    lax.fori_loop(0, MODES, place, 0)
     first = jnp.concatenate([terms[a] for a in range(4)], axis=1)
     second = jnp.concatenate([terms[a + 4] for a in range(4)], axis=1)
     hi, lo = split(jnp.concatenate([first + second, first - second], axis=0))
@@ -433,34 +478,38 @@
     top = iota((1, 8, 1), 1) < KL
 
     def inverse(n, carry):
-        j = lax.rem(rad + n, 6)
-        ib = j + j // 3
-        block = pl.ds(pl.multiple_of(ib * 128, 128), 128)
-        th, tl = table_hi[block, :], table_lo[block, :]
-        out = mm_nt(splits[0], th) + mm_nt(splits[1], th) + mm_nt(splits[0], tl)
-        chosen = jnp.where(parity, out[: 2 * ROWS], out[2 * ROWS :]).reshape(HB, 2, 8, 128)
-        even, odd = chosen[:, 0], chosen[:, 1]
-        real = jnp.where(top, even, pltpu.roll(odd, 4, 1))
-        imag = jnp.where(top, pltpu.roll(even, 4, 1), odd)
-        spectral[rows(ib), :] = real.reshape(ROWS, 128)
-        spectral[rows(8 + ib), :] = imag.reshape(ROWS, 128)
-        for c in range(2):
-            d = lax.rem(c * 8 + ib - rad + RADS, RADS)
-
-            @pl.when(d > 0)
-            def _():
-                back_copy(d).start()
-
-            @pl.when(d == 0)
-            def _():
-                own_back.start()
+        line = lax.rem(y + n // 2 + 2, 4)
+
+        @pl.when(line != 3)
+        def _():
+            ib = lax.rem(x + n, 2) * 4 + line
+            block = pl.ds(pl.multiple_of(ib * 128, 128), 128)
+            th, tl = table_hi[block, :], table_lo[block, :]
+            out = mm_nt(splits[0], th) + mm_nt(splits[1], th) + mm_nt(splits[0], tl)
+            chosen = jnp.where(parity, out[: 2 * ROWS], out[2 * ROWS :]).reshape(HB, 2, 8, 128)
+            even, odd = chosen[:, 0], chosen[:, 1]
+            real = jnp.where(top, even, pltpu.roll(odd, 4, 1))
+            imag = jnp.where(top, pltpu.roll(even, 4, 1), odd)
+            spectral[rows(ib), :] = real.reshape(ROWS, 128)
+            spectral[rows(8 + ib), :] = imag.reshape(ROWS, 128)
+            for c in range(2):
+                dx = lax.rem(2 * c + ib // 4 - x + 4, 4)
+                d = dx * 4 + lax.rem(line - y + 4, 4)
+
+                @pl.when(d > 0)
+                def _():
+                    back_copy(d).start()
+
+                @pl.when(d == 0)
+                def _():
+                    own_back.start()
 
         return carry
 
     own_back = pltpu.make_async_copy(
         spectral.at[rows(rad)], returned.at[rows(rad)], stores.at[2]
     )
-    lax.fori_loop(0, 6, inverse, 0)
+    lax.fori_loop(0, 8, inverse, 0)
     takes = lax.rem(rad, 4) != 3
     for copy in kept:
         copy.wait()
@@ -469,8 +518,12 @@
         field_copy(d).wait_send()
     for d in range(1, MODES):
         gather_copy(d).wait_send()
-        reduce_copy(d).wait_send()
-        push_back(d).wait_send()
+    for o in range(4):
+        twin_part(o).wait_send()
+        push_copy_twin(o).wait_send()
+        if o:
+            reduce_copy(o).wait_send()
+            push_copy_above(o).wait_send()
     for d in range(1, RADS):
         @pl.when(lax.rem(rad_peer(d), 4) != 3)
         def _():
@@ -496,7 +549,7 @@
     return lower, upper, centre, radius * radius
 
 
-def solve_body(returned, known, keep, g_ref, nxt, forcing, rhs, work):
+def solve_body(returned, known, keep, g_ref, nxt_out, forcing_out, rhs, work, nxt, forcing, sems):
     rad = lax.axis_index("rad")
     half = RADII // 2
     lane = lax.rem(rad, 8) * 128 + iota((8, 128), 1)
@@ -508,9 +561,16 @@
     kept_here = m <= most
     top = sub < KL
     gain = time_step * gamma_rk
+    scale = -implicit * RADII * RADII
+    slope = jnp.where(top, 1.0, -1.0)
+    outer_start = jnp.where(top, 0.0, scale * RADII)
+    inner_start = jnp.where(top, scale, scale * (RADII - 1))
 
     def rows(q):
         return pl.ds(pl.multiple_of(q * 8, 8), 8)
+
+    def weighed(j):
+        return (jnp.where(top, 0.5, RADII - 0.5) + slope * j.astype(F32)) * g_ref[j]
 
     def fold(q, carry):
         sides = []
@@ -518,44 +578,40 @@
             kept = jnp.where(kept_here, returned[rows(n), :], 0.0)
             rhs[rows(n), :] = kept
             sides.append(known[rows(n), :] + gain * kept)
-        work[2 * q] = jnp.where(top, sides[0], sides[1]) * g_ref[2 * q]
+        work[2 * q] = jnp.where(top, sides[0], sides[1]) * weighed(2 * q)
         odd = pltpu.roll(jnp.where(top, sides[1], sides[0]), 4, 0)
-        work[2 * q + 1] = odd * g_ref[2 * q + 1]
+        work[2 * q + 1] = odd * weighed(2 * q + 1)
         return carry
+
+    def save(n, k, src, dst):
+        return pltpu.make_async_copy(src.at[k], dst.at[k], sems.at[n, k])
 
     lax.fori_loop(0, half // 2, fold, 0, unroll=8)
     for k in range(KL):
         forcing[k] = jnp.transpose(rhs[pl.ds(k, RADII, stride=KL), :])
-
-    scale = -implicit * RADII * RADII
-
-    def couplings(j):
-        r = jnp.where(top, j, RADII - 1 - j)
-        off = r.astype(F32)
-        inverse = scale / (off + 0.5)
-        after = jnp.where(r == RADII - 1, 0.0, off + 1.0)
-        return jnp.where(top, off, after) * inverse, jnp.where(top, after, off) * inverse
+        save(0, k, forcing, forcing_out).start()
 
     def down(j, d):
-        outer, _ = couplings(j)
-        d = work[j] - (outer * g_ref[j]) * d
+        d = work[j] - ((outer_start + (scale * slope) * j.astype(F32)) * g_ref[j]) * d
         work[j] = d
         return d
 
-    d = lax.fori_loop(0, half, down, jnp.zeros((8, 128), F32), unroll=8)
-    _, inner = couplings(half - 1)
-    v = inner * g_ref[half - 1]
+    d = lax.fori_loop(0, half, down, jnp.zeros((8, 128), F32), unroll=16)
+
+    def inner(j):
+        return (inner_start + (scale * slope) * j.astype(F32)) * g_ref[j]
+
+    v = inner(jnp.int32(half - 1))
     x = (d - v * pltpu.roll(d, 4, 0)) / (1.0 - v * pltpu.roll(v, 4, 0))
     work[half - 1] = x
 
     def back(n, x):
         j = half - 2 - n
-        _, inner = couplings(j)
-        x = work[j] - (inner * g_ref[j]) * x
+        x = work[j] - inner(j) * x
         work[j] = x
         return x
 
-    lax.fori_loop(0, half - 1, back, x, unroll=8)
+    lax.fori_loop(0, half - 1, back, x, unroll=16)
 
     def unfold(q, carry):
         even = work[2 * q]
@@ -567,9 +623,14 @@
     lax.fori_loop(0, half // 2, unfold, 0, unroll=8)
     for k in range(KL):
         nxt[k] = jnp.transpose(rhs[pl.ds(k, RADII, stride=KL), :])
-
-
-def vmem_call(body, outs, n_in, scratch, collective=None, smem=(), name=None, space=VMEM):
+        save(1, k, nxt, nxt_out).start()
+    for k in range(KL):
+        save(0, k, forcing, forcing_out).wait()
+        save(1, k, nxt, nxt_out).wait()
+
+
+def vmem_call(body, outs, n_in, scratch, collective=None, smem=(), name=None, space=VMEM,
+    out_space=None):
     spec = [
         pl.BlockSpec(memory_space=pltpu.SMEM if n in smem else space) for n in range(n_in)
     ]
@@ -580,7 +641,7 @@
         body,
         out_shape=[jax.ShapeDtypeStruct(s, F32) for s in outs],
         in_specs=spec,
-        out_specs=[pl.BlockSpec(memory_space=space)] * len(outs),
+        out_specs=[pl.BlockSpec(memory_space=out_space or space)] * len(outs),
         scratch_shapes=scratch,
         compiler_params=pltpu.CompilerParams(**params),
         name=name,
@@ -645,12 +706,15 @@
             VMEM((2 * ROWS, RADS * CAP), BF16),
             VMEM((2, 4 * ROWS, HALF), BF16),
             VMEM(slots, F32),
-            VMEM(slots, F32),
+            VMEM((4, RADS, CAP), F32),
+            VMEM((4, RADS, CAP), F32),
+            VMEM((4, RADS, CAP), F32),
             VMEM(slots, F32),
             DMA((11,)), DMA((3,)),
             DMA((RADS,)), DMA((RADS,)), DMA((RADS,)), DMA((RADS,)),
-            DMA((MODES,)), DMA((MODES,)), DMA((MODES,)), DMA((MODES,)),
-            DMA((MODES,)), DMA((MODES,)), DMA((RADS,)), DMA((RADS,)),
+            DMA((MODES,)), DMA((MODES,)),
+            DMA((4,)), DMA((4,)), DMA((4,)), DMA((4,)), DMA((4,)), DMA((4,)), DMA((4,)), DMA((4,)),
+            DMA((RADS,)), DMA((RADS,)),
         ],
         collective=0,
         name="substep",
@@ -663,9 +727,16 @@
         solve_body,
         [(KL, 128, RADII), (KL, 128, RADII)],
         4,
-        [VMEM(all_rows, F32), VMEM(tiles, F32)],
+        [
+            VMEM(all_rows, F32),
+            VMEM(tiles, F32),
+            VMEM(field_coef.shape, F32),
+            VMEM(field_coef.shape, F32),
+            DMA((2, KL)),
+        ],
         smem=(2,),
         name="solve",
+        out_space=pl.ANY,
     )(returned, known, keep_modes, g)
     return (field_next, forcing)
 

time: 60.9 us -> 57.9 us (0.951); the launches traced: 60.1 us -> 57.8 us
  Pallas kernels: 59.4 us -> 57.1 us
    pallas_call x1, Pallas kernels: 54.3 us -> 52.3 us  [per_device(): vmem_call(substep_body, [all_rows, all_rows, tiles], 11, [VMEM(field_coef...]
where the time goes in v3:
time: 57.9 us; the launch traced here: 57.8 us
  Pallas kernels  57.1 us (99%)
  between operations  0.64 us (1%)
    pallas_call x1, Pallas kernels, per_device(): vmem_call(substep_body, [all_rows, all_rows, tiles], 11, [VMEM(field_coef...  52.3 us
    pallas_call x1, Pallas kernels, per_device(): vmem_call(solve_body, [(KL, 128, RADII), (KL, 128, RADII)], 4, [VMEM(all_...  4.81 us

profile of v3, /device:TPU:1, one launch (start us, length us, event | category | flops | bytes accessed | tf_op | source)
XLA Modules:
  0.0 57.8 jit_solution(11375191901263156368)
XLA Ops:
  0.6 52.3 %substep.1 = (f32[1536,128]{1,0:T(8,128)}, f32[1536,128]{1,0:T(8,128)}, f32[192,8,128]{2,1,0:T(8,128)}) custom-call(f32[4,128,384]{2,1,0:T(8,128)} %field_in.1, f32[4,128,384]{2,1,0:T(8,128)} %prior_in.1, f32[24,1024]{1,0:T(8,128)} %base_in.1, s32[1,2048]{1,0:T(1,128)} %bitcast.6, s32[1,2048]{1,0:T(1,128)} %bitcast.7, f32[1,2048]{1,0:T(1,128)} %bitcast.8, ...), custom_call_target="tpu_custom_call" | custom-call | tf_op jit(solution)/shard_map/substep/pallas_call | solution.py:675
  53.0 4.8 %solve.1 = (f32[4,128,384]{2,1,0:T(8,128)}, f32[4,128,384]{2,1,0:T(8,128)}) custom-call(f32[1536,128]{1,0:T(8,128)} %get-tuple-element.5.returned, f32[1536,128]{1,0:T(8,128)} %get-tuple-element.6.known, s32[4]{0:T(128)} %keep.1, f32[192,8,128]{2,1,0:T(8,128)} %get-tuple-element.7.g_ref), custom_call_target="tpu_custom_call" | custom-call | tf_op jit(solution)/shard_map/solve/pallas_call | solution.py:726

commit v4 on v3

--- a/solution.py
+++ b/solution.py
@@ -70,12 +70,11 @@
     barrier = pltpu.get_barrier_semaphore()
     mode, rad = lax.axis_index("mode"), lax.axis_index("rad")
     if rad_peers:
-        for d in range(1, RADS):
-            pl.semaphore_signal(
-                barrier, inc=1, device_id=(mode, lax.rem(rad + d, RADS)), device_id_type=MESH
-            )
+        for d in NEAR[::-1]:
+            there = lax.rem(rad // 4 + d // 4, 4) * 4 + lax.rem(lax.rem(rad, 4) + d % 4, 4)
+            pl.semaphore_signal(barrier, inc=1, device_id=(mode, there), device_id_type=MESH)
     if mode_peers:
-        for d in range(1, MODES):
+        for d in (4, 5, 3, 2, 6, 7, 1):
             pl.semaphore_signal(
                 barrier, inc=1, device_id=(lax.rem(mode + d, MODES), rad), device_id_type=MESH
             )
@@ -246,13 +245,13 @@
     for s in range(RADS):
         _, rh = cell_parts(gathered[m, s : s + 1, :])
         value = pushes[m, s : s + 1, :] * weights[m, s]
-        high = value.astype(BF16).astype(F32)
-        low = value - high
-        rows = [jnp.where(rh == q, high, 0.0) for q in range(HB)]
-        rows += [jnp.where(rh == q, low, 0.0) for q in range(HB)]
-        masses[:, s * CAP : (s + 1) * CAP] = jnp.concatenate(rows, axis=0).astype(BF16)
-    both = mm_nt(masses[...], onehots[m])
-    deposit = both[:ROWS] + both[ROWS:]
+        tile = jnp.concatenate(split(value), axis=0)
+        place = jnp.broadcast_to(rh.astype(BF16), (16, CAP))
+        masses[:, s * CAP : (s + 1) * CAP] = jnp.concatenate(
+            [jnp.where(place == q, tile, jnp.zeros((), BF16)) for q in range(HB)], axis=0
+        )
+    both = mm_nt(masses[...], onehots[m]).reshape(HB, 2, 8, 256)
+    deposit = (both[:, 0] + both[:, 1]).reshape(ROWS, 256)
     for h in range(2):
         rows = slice(h * ROWS, (h + 1) * ROWS)
         terms[m, rows, :] = terms[m, rows, :] + deposit[:, h * 128 : (h + 1) * 128]
@@ -406,23 +405,25 @@
         t = lax.rem(n + 2, 4)
         return t + (n // 2) * (1 - 2 * t)
 
-    def sample_twin(n, carry):
-        o = outward(n)
-        m = lax.rem(z + o, 4) * 2 + 1 - core
+    def sample(n, carry):
+        mine = jnp.where((n == 2) | (n == 4) | (n == 5) | (n == 7), 1, 0)
+        late = jnp.where(n > 2, 1, 0) + jnp.where(n > 4, 1, 0) + jnp.where(n > 5, 1, 0)
+        o = outward(mine * late + (1 - mine) * (n - late))
+        m = lax.rem(z + o, 4) * 2 + lax.rem(core + 1 - mine, 2)
         sample_arc(m, grid, gathered, onehots, weights, partial)
-        twin_part(o).start()
-        return carry
-
-    def sample_own(n, carry):
-        o = outward(n)
-        m = above(o)
-        sample_arc(m, grid, gathered, onehots, weights, partial)
-        twin_part(o).wait_recv()
-        totals[o] = partial[m] + twins[o]
-
-        @pl.when(o > 0)
-        def _():
-            reduce_copy(o).start()
+
+        @pl.when(mine == 0)
+        def _():
+            twin_part(o).start()
+
+        @pl.when(mine == 1)
+        def _():
+            twin_part(o).wait_recv()
+            totals[o] = partial[m] + twins[o]
+
+            @pl.when(o > 0)
+            def _():
+                reduce_copy(o).start()
 
         return carry
 
@@ -430,8 +431,7 @@
         advect_arc(m, mode, grid, flow, terms)
         return carry
 
-    lax.fori_loop(0, 4, sample_twin, 0)
-    lax.fori_loop(0, 4, sample_own, 0)
+    lax.fori_loop(0, MODES, sample, 0)
     lax.fori_loop(0, MODES, advect, 0)
     for o in (1, 3, 2):
         reduce_copy(o).wait_recv()

time: 57.9 us -> 57.2 us (0.988)
  Pallas kernels: 57.1 us -> 56.4 us
    pallas_call x1, Pallas kernels: 52.3 us -> 51.6 us  [per_device(): vmem_call(substep_body, [all_rows, all_rows, tiles], 11, [VMEM(field_coef...]
where the time goes in v4:
time: 57.2 us; the launch traced here: 57.1 us
  Pallas kernels  56.4 us (99%)
  between operations  0.64 us (1%)
    pallas_call x1, Pallas kernels, per_device(): vmem_call(substep_body, [all_rows, all_rows, tiles], 11, [VMEM(field_coef...  51.6 us
    pallas_call x1, Pallas kernels, per_device(): vmem_call(solve_body, [(KL, 128, RADII), (KL, 128, RADII)], 4, [VMEM(all_...  4.81 us

profile of v4, /device:TPU:1, one launch (start us, length us, event | category | flops | bytes accessed | tf_op | source)
XLA Modules:
  0.0 57.1 jit_solution(10186760920707324704)
XLA Ops:
  0.6 51.6 %substep.1 = (f32[1536,128]{1,0:T(8,128)}, f32[1536,128]{1,0:T(8,128)}, f32[192,8,128]{2,1,0:T(8,128)}) custom-call(f32[4,128,384]{2,1,0:T(8,128)} %field_in.1, f32[4,128,384]{2,1,0:T(8,128)} %prior_in.1, f32[24,1024]{1,0:T(8,128)} %base_in.1, s32[1,2048]{1,0:T(1,128)} %bitcast.6, s32[1,2048]{1,0:T(1,128)} %bitcast.7, f32[1,2048]{1,0:T(1,128)} %bitcast.8, ...), custom_call_target="tpu_custom_call" | custom-call | tf_op jit(solution)/shard_map/substep/pallas_call | solution.py:675
  52.3 4.8 %solve.1 = (f32[4,128,384]{2,1,0:T(8,128)}, f32[4,128,384]{2,1,0:T(8,128)}) custom-call(f32[1536,128]{1,0:T(8,128)} %get-tuple-element.5.returned, f32[1536,128]{1,0:T(8,128)} %get-tuple-element.6.known, s32[4]{0:T(128)} %keep.1, f32[192,8,128]{2,1,0:T(8,128)} %get-tuple-element.7.g_ref), custom_call_target="tpu_custom_call" | custom-call | tf_op jit(solution)/shard_map/solve/pallas_call | solution.py:726

commit v5 on v4

--- a/solution.py
+++ b/solution.py
@@ -478,7 +478,7 @@
     top = iota((1, 8, 1), 1) < KL
 
     def inverse(n, carry):
-        line = lax.rem(y + n // 2 + 2, 4)
+        line = lax.rem(y + n // 2 + 0, 4)
 
         @pl.when(line != 3)
         def _():

time: 57.2 us -> 56.2 us (0.983)
  Pallas kernels: 56.4 us -> 55.4 us
    pallas_call x1, Pallas kernels: 51.6 us -> 50.6 us  [per_device(): vmem_call(substep_body, [all_rows, all_rows, tiles], 11, [VMEM(field_coef...]
where the time goes in v5:
time: 56.2 us; the launch traced here: 56 us
  Pallas kernels  55.4 us (99%)
  between operations  0.64 us (1%)
    pallas_call x1, Pallas kernels, per_device(): vmem_call(substep_body, [all_rows, all_rows, tiles], 11, [VMEM(field_coef...  50.6 us
    pallas_call x1, Pallas kernels, per_device(): vmem_call(solve_body, [(KL, 128, RADII), (KL, 128, RADII)], 4, [VMEM(all_...  4.81 us

profile of v5, /device:TPU:1, one launch (start us, length us, event | category | flops | bytes accessed | tf_op | source)
XLA Modules:
  0.0 56.0 jit_solution(11930075024376268826)
XLA Ops:
  0.6 50.6 %substep.1 = (f32[1536,128]{1,0:T(8,128)}, f32[1536,128]{1,0:T(8,128)}, f32[192,8,128]{2,1,0:T(8,128)}) custom-call(f32[4,128,384]{2,1,0:T(8,128)} %field_in.1, f32[4,128,384]{2,1,0:T(8,128)} %prior_in.1, f32[24,1024]{1,0:T(8,128)} %base_in.1, s32[1,2048]{1,0:T(1,128)} %bitcast.6, s32[1,2048]{1,0:T(1,128)} %bitcast.7, f32[1,2048]{1,0:T(1,128)} %bitcast.8, ...), custom_call_target="tpu_custom_call" | custom-call | tf_op jit(solution)/shard_map/substep/pallas_call | solution.py:675
  51.2 4.8 %solve.1 = (f32[4,128,384]{2,1,0:T(8,128)}, f32[4,128,384]{2,1,0:T(8,128)}) custom-call(f32[1536,128]{1,0:T(8,128)} %get-tuple-element.5.returned, f32[1536,128]{1,0:T(8,128)} %get-tuple-element.6.known, s32[4]{0:T(128)} %keep.1, f32[192,8,128]{2,1,0:T(8,128)} %get-tuple-element.7.g_ref), custom_call_target="tpu_custom_call" | custom-call | tf_op jit(solution)/shard_map/solve/pallas_call | solution.py:726

commit v6 on v5

--- a/solution.py
+++ b/solution.py
@@ -432,7 +432,7 @@
         return carry
 
     lax.fori_loop(0, MODES, sample, 0)
-    lax.fori_loop(0, MODES, advect, 0)
+    lax.fori_loop(0, MODES // 2, advect, 0)
     for o in (1, 3, 2):
         reduce_copy(o).wait_recv()
     fluid = (totals[0] + parts[1]) + (parts[2] + parts[3])
@@ -441,6 +441,7 @@
     for o in (2, 3, 1):
         push_copy_above(o).start()
     push_copy_twin(0).start()
+    lax.fori_loop(MODES // 2, MODES, advect, 0)
 
     def arrive(o):
         push_copy_above(o).wait_recv()

time: 56.2 us -> 56.2 us (level)
  no operation moved by 1% of the time
where the time goes in v6:
time: 56.2 us; the launch traced here: 56 us
  Pallas kernels  55.4 us (99%)
  between operations  0.64 us (1%)
    pallas_call x1, Pallas kernels, per_device(): vmem_call(substep_body, [all_rows, all_rows, tiles], 11, [VMEM(field_coef...  50.6 us
    pallas_call x1, Pallas kernels, per_device(): vmem_call(solve_body, [(KL, 128, RADII), (KL, 128, RADII)], 4, [VMEM(all_...  4.81 us

profile of v6, /device:TPU:1, one launch (start us, length us, event | category | flops | bytes accessed | tf_op | source)
XLA Modules:
  0.0 56.0 jit_solution(361272647387727945)
XLA Ops:
  0.6 50.6 %substep.1 = (f32[1536,128]{1,0:T(8,128)}, f32[1536,128]{1,0:T(8,128)}, f32[192,8,128]{2,1,0:T(8,128)}) custom-call(f32[4,128,384]{2,1,0:T(8,128)} %field_in.1, f32[4,128,384]{2,1,0:T(8,128)} %prior_in.1, f32[24,1024]{1,0:T(8,128)} %base_in.1, s32[1,2048]{1,0:T(1,128)} %bitcast.6, s32[1,2048]{1,0:T(1,128)} %bitcast.7, f32[1,2048]{1,0:T(1,128)} %bitcast.8, ...), custom_call_target="tpu_custom_call" | custom-call | tf_op jit(solution)/shard_map/substep/pallas_call | solution.py:676
  51.2 4.8 %solve.1 = (f32[4,128,384]{2,1,0:T(8,128)}, f32[4,128,384]{2,1,0:T(8,128)}) custom-call(f32[1536,128]{1,0:T(8,128)} %get-tuple-element.5.returned, f32[1536,128]{1,0:T(8,128)} %get-tuple-element.6.known, s32[4]{0:T(128)} %keep.1, f32[192,8,128]{2,1,0:T(8,128)} %get-tuple-element.7.g_ref), custom_call_target="tpu_custom_call" | custom-call | tf_op jit(solution)/shard_map/solve/pallas_call | solution.py:727
